TPU v7x, 32 devices: a whole 2x2x4 slice. The times are simulated.
32 devices in a mesh: segment: 4 (over y, x), gy: 8 (over z, core).
Axes of the slice: x: 2, y: 2, z: 4, core: 2. Of those that a mesh axis runs over, the one named last changes fastest.
Arguments:
- crops: bfloat16 [2, 32, 4, 32, 128], P(None, None, None, 'gy'), may hold values from -6 to 6
- cotangent: bfloat16 [2, 32, 4, 32, 128], P(None, None, None, 'gy'), may hold values from -0.59765625 to 0.59765625
- weights: bfloat16 [4, 2, 27, 32, 32], P('segment'), may hold values from -0.375 to 0.375
Outputs:
- features: bfloat16 [4, 2, 32, 4, 32, 128], P('segment', None, None, None, 'gy')
- weight_grads: float32 [4, 2, 27, 32, 32], P('segment')
- input_grads: float32 [4, 2, 32, 4, 32, 128], P('segment', None, None, None, 'gy')
All inputs are finite; a program needn't handle non-finite values.
Results may differ from a plain program's by a relative error of at most 0.025.
Values may be sent and summed in bfloat16 or wider, within the bound.
A program may use at most 128 MiB of HBM per device.

v0:
```python
import jax
import jax.numpy as jnp
from jax import lax
from jax.sharding import PartitionSpec as P


def extended(block, sides, width):
    for axis, dim in sides:
        count = lax.axis_size(axis)
        forward = [(i, i + 1) for i in range(count - 1)]
        backward = [(target, source) for source, target in forward]
        low = lax.ppermute(
            lax.slice_in_dim(block, block.shape[dim] - width, None, axis=dim), axis, forward
        )
        high = lax.ppermute(lax.slice_in_dim(block, 0, width, axis=dim), axis, backward)
        block = jnp.concatenate([low, block, high], axis=dim)
    return block


def from_partner(array, axis, bit):
    return lax.ppermute(array, axis, [(i, i ^ 1 << bit) for i in range(lax.axis_size(axis))])


def passed_along(value, axis, steps):
    count = lax.axis_size(axis)
    first, last = (max(0, -steps), min(count, count - steps))
    return lax.ppermute(value, axis, [(source, source + steps) for source in range(first, last)])


def slices_of(padded, plane_shift, row_count):
    planes = padded.shape[1] - 2
    across = padded.shape[3] - 2
    return jnp.stack(
        [
            padded[
                :,
                plane_shift : plane_shift + planes,
                row_shift : row_shift + row_count,
                side_shift : side_shift + across,
            ]
            for row_shift in range(3)
            for side_shift in range(3)
        ]
    )


def convolve(padded, kernel, row_count):
    result = None
    for plane_shift in range(3):
        contribution = jnp.einsum(
            "tczyx,tco->ozyx",
            slices_of(padded, plane_shift, row_count),
            kernel[9 * plane_shift : 9 * plane_shift + 9],
            preferred_element_type=jnp.float32,
        )
        result = contribution if result is None else result + contribution
    return result


def kernel_grads(padded, gradient, row_count):
    pieces = []
    for plane_shift in range(3):
        pieces.append(
            jnp.einsum(
                "tczyx,ozyx->tco",
                slices_of(padded, plane_shift, row_count),
                gradient,
                preferred_element_type=jnp.float32,
            )
        )
    return jnp.concatenate(pieces, 0)


def flipped(kernel):
    return jnp.transpose(jnp.flip(kernel, 0), (0, 2, 1))


def slope(preact):
    logistic = jax.nn.sigmoid(preact)
    return logistic * (1.0 + preact * (1.0 - logistic))


def side_pad(volume):
    return jnp.pad(volume, ((0, 0), (1, 1), (0, 0), (1, 1)))


def gradient_rows(volume):
    return side_pad(extended(volume, (("gy", 2),), 1))


def mirror_forward(volume):
    for bit_number in range(2):
        volume = from_partner(volume, "segment", bit_number)
    return volume


def mirror_backward(volume):
    for bit_number in range(2):
        volume = from_partner(volume, "segment", bit_number)
    return volume


def pick(buffer, slot_index):
    return lax.dynamic_index_in_dim(buffer, slot_index, 0, keepdims=False)


def place(buffer, value, slot_index, active):
    return lax.dynamic_update_index_in_dim(
        buffer, jnp.where(active, value, pick(buffer, slot_index)), slot_index, 0
    )


def local(crops, cotangent, weights):
    micro_count, channels, planes, row_count, across = crops.shape
    segment_index = lax.axis_index("segment")
    row_offset = lax.axis_index("gy") * row_count
    all_rows = lax.axis_size("gy") * row_count
    moments = micro_count + 3
    kernel_first = weights[0, 0]
    kernel_second = weights[0, 1]
    block = (channels, planes, row_count, across)
    empty_block = jnp.zeros(block, jnp.bfloat16)
    padded_shape = (micro_count, channels, planes + 2, row_count + 2, across + 2)
    input_store = jnp.zeros(padded_shape, jnp.bfloat16)
    hidden_store = jnp.zeros(padded_shape, jnp.bfloat16)
    first_store = jnp.zeros((micro_count,) + block, jnp.float32)
    second_store = jnp.zeros((micro_count,) + block, jnp.float32)
    feature_store = jnp.zeros((micro_count,) + block, jnp.bfloat16)
    skip_store = jnp.zeros((micro_count,) + block, jnp.bfloat16)
    from_before = empty_block
    for moment in range(moments):
        position = moment - segment_index
        active = (position >= 0) & (position < micro_count)
        slot_index = jnp.clip(position, 0, micro_count - 1)
        entering = jnp.where(segment_index == 0, pick(crops, slot_index), from_before)
        skip_rows = pick(skip_store, slot_index)
        merged = jnp.where(
            segment_index >= 2,
            (entering.astype(jnp.float32) + skip_rows.astype(jnp.float32)).astype(jnp.bfloat16),
            entering,
        )
        widened = side_pad(extended(merged, (("gy", 2),), 2))
        pre_wide = convolve(widened, kernel_first, row_count + 2)
        global_rows = row_offset - 1 + jnp.arange(row_count + 2)
        inside = ((global_rows >= 0) & (global_rows < all_rows))[None, None, :, None]
        hidden_pad = side_pad(jnp.where(inside, jax.nn.silu(pre_wide), 0.0).astype(jnp.bfloat16))
        input_pad = widened[:, :, 1:-1]
        pre_first = pre_wide[:, :, 1:-1]
        pre_second = convolve(hidden_pad, kernel_second, row_count)
        leaving = jax.nn.silu(pre_second).astype(jnp.bfloat16)
        input_store = place(input_store, input_pad, slot_index, active)
        hidden_store = place(hidden_store, hidden_pad, slot_index, active)
        first_store = place(first_store, pre_first, slot_index, active)
        second_store = place(second_store, pre_second, slot_index, active)
        feature_store = place(feature_store, leaving, slot_index, active)
        if moment + 1 < moments:
            arrived_position = moment - (3 - segment_index)
            arrived = (
                (arrived_position >= 0) & (arrived_position < micro_count) & (segment_index >= 2)
            )
            skip_store = place(
                skip_store,
                mirror_forward(entering),
                jnp.clip(arrived_position, 0, micro_count - 1),
                arrived,
            )
            from_before = passed_along(leaving, "segment", 1)
    flip_first = flipped(kernel_first)
    flip_second = flipped(kernel_second)
    grad_sum = jnp.zeros((2,) + kernel_first.shape, jnp.float32)
    grad_store = jnp.zeros((micro_count,) + block, jnp.bfloat16)
    input_grads = jnp.zeros((micro_count,) + block, jnp.float32)
    from_after = empty_block
    for moment in range(moments):
        position = moment - (3 - segment_index)
        active = (position >= 0) & (position < micro_count)
        slot_index = jnp.clip(position, 0, micro_count - 1)
        incoming = jnp.where(segment_index == 3, pick(cotangent, slot_index), from_after)
        second_delta = (
            incoming.astype(jnp.float32) * slope(pick(second_store, slot_index))
        ).astype(jnp.bfloat16)
        grad_second = kernel_grads(pick(hidden_store, slot_index), second_delta, row_count)
        hidden_delta = convolve(gradient_rows(second_delta), flip_second, row_count)
        first_delta = (hidden_delta * slope(pick(first_store, slot_index))).astype(jnp.bfloat16)
        grad_first = kernel_grads(pick(input_store, slot_index), first_delta, row_count)
        grad_sum = grad_sum + jnp.where(active, jnp.stack([grad_first, grad_second]), 0.0)
        delta = convolve(gradient_rows(first_delta), flip_first, row_count).astype(jnp.bfloat16)
        extra = pick(grad_store, slot_index)
        summed = delta.astype(jnp.float32) + extra.astype(jnp.float32)
        input_grads = place(input_grads, summed, slot_index, active)
        passing = jnp.where(segment_index == 1, summed.astype(jnp.bfloat16), delta)
        if moment + 1 < moments:
            arrived_position = moment - segment_index
            arrived = (
                (arrived_position >= 0) & (arrived_position < micro_count) & (segment_index <= 1)
            )
            grad_store = place(
                grad_store,
                mirror_backward(delta),
                jnp.clip(arrived_position, 0, micro_count - 1),
                arrived,
            )
            from_after = passed_along(passing, "segment", -1)
    weight_grads = lax.psum(grad_sum.astype(jnp.bfloat16), "gy").astype(jnp.float32)
    return (feature_store[None], weight_grads[None], input_grads[None])


def solution(mesh):
    return jax.shard_map(
        local,
        mesh=mesh,
        in_specs=(
            P(None, None, None, "gy", None),
            P(None, None, None, "gy", None),
            P("segment", None, None, None, None),
        ),
        out_specs=(
            P("segment", None, None, None, "gy", None),
            P("segment", None, None, None, None),
            P("segment", None, None, None, "gy", None),
        ),
        check_vma=False,
    )
```

profile of v0, /device:TPU:0, one launch (start us, length us, event | category | flops | bytes accessed | tf_op | source)
XLA Modules:
  0.0 362.3 jit_solution(7427069599511536206)
XLA Ops:
  7.2 1.4 constant_dynamic-slice_fusion.38
  8.7 3.0 collective-permute-start.3
  11.8 1.5 collective-permute-start
  13.2 1.3 collective-permute-start.1
  15.1 3.0 collective-permute-done.1
  26.1 2.4 collective-permute-start.2
  29.5 1.6 collective-permute-start.4
  31.1 5.4 %collective-permute-done.4 = bf16[32,4,4,128]{3,0,2,1:T(8,128)(2,1)S(1)} collective-permute-done((bf16[32,4,4,128]{3,0,2,1:T(8,128)(2,1)S(1)}, bf16[32,4,4,128]{3,0,2,1:T(8,128)(2,1)S(1)}, u32[]{:S(2)}, u32[]{:S(2)}) %collective-permute-start.4) | collective-permute-done | bytes 131104 | tf_op jit(solution)/shard_map/ppermute | solution.py:21
  36.7 2.7 collective-permute-start.5
  39.4 1.5 collective-permute-start.6
  42.1 2.6 collective-permute-done.6
  52.8 2.7 collective-permute-start.7
  56.2 1.8 collective-permute-start.9
  58.1 6.1 %collective-permute-done.9 = bf16[32,4,4,128]{3,0,2,1:T(8,128)(2,1)S(1)} collective-permute-done((bf16[32,4,4,128]{3,0,2,1:T(8,128)(2,1)S(1)}, bf16[32,4,4,128]{3,0,2,1:T(8,128)(2,1)S(1)}, u32[]{:S(2)}, u32[]{:S(2)}) %collective-permute-start.9) | collective-permute-done | bytes 131104 | tf_op jit(solution)/shard_map/ppermute | solution.py:21
  64.3 2.6 collective-permute-start.10
  66.9 1.3 collective-permute-start.11
  69.4 3.0 collective-permute-done.11
  80.5 2.9 collective-permute-start.12
  84.1 2.0 collective-permute-start.14
  86.1 5.7 %collective-permute-done.14 = bf16[32,4,4,128]{3,0,2,1:T(8,128)(2,1)S(1)} collective-permute-done((bf16[32,4,4,128]{3,0,2,1:T(8,128)(2,1)S(1)}, bf16[32,4,4,128]{3,0,2,1:T(8,128)(2,1)S(1)}, u32[]{:S(2)}, u32[]{:S(2)}) %collective-permute-start.14) | collective-permute-done | bytes 131104 | tf_op jit(solution)/shard_map/ppermute | solution.py:21
  92.0 2.7 collective-permute-start.15
  94.7 1.3 collective-permute-start.16
  96.0 1.5 collective-permute-start.18
  97.5 2.5 collective-permute-done.16
  108.7 2.5 collective-permute-start.19
  111.2 1.3 collective-permute-start.17
  112.6 1.5 collective-permute-done.19
  115.1 4.1 %collective-permute-start.20 = (bf16[32,4,2,128]{3,0,2,1:T(8,128)(2,1)S(1)}, bf16[32,4,2,128]{3,0,2,1:T(8,128)(2,1)S(1)}, u32[]{:S(2)}, u32[]{:S(2)}) collective-permute-start(bf16[32,4,2,128]{3,0,2,1:T(8,128)(2,1)S(1)} %get-tuple-element.615), channel_id=1, source_target_pairs={{0,1},{1,2},{2,3},{3,4},{4,5},{5,6},{6,7},{8,9},{9,10},{10,11},{11... | collective-permute-start | bytes 196616 | tf_op jit(solution)/shard_map/ppermute | solution.py:12
  119.2 1.3 collective-permute-start.21
  120.6 2.8 collective-permute-done.21
  131.4 4.8 %collective-permute-start.22 = (bf16[32,4,1,128]{3,0,2,1:T(8,128)(2,1)S(1)}, bf16[32,4,1,128]{3,0,2,1:T(8,128)(2,1)S(1)}, u32[]{:S(2)}, u32[]{:S(2)}) collective-permute-start(bf16[32,4,1,128]{3,0,2,1:T(8,128)(2,1)S(1)} %get-tuple-element.613), channel_id=1, source_target_pairs={{0,1},{1,2},{2,3},{3,4},{4,5},{5,6},{6,7},{8,9},{9,10},{10,11},{11... | collective-permute-start | bytes 98312 | tf_op jit(solution)/shard_map/ppermute | solution.py:12
  136.3 1.5 collective-permute-start.23
  164.0 3.0 collective-permute-start.24
  167.0 1.3 collective-permute-start.25
  174.1 1.3 collective-permute-start.26
  175.5 3.1 collective-permute-start.31
  178.6 2.8 collective-permute-done.26
  181.6 4.5 %collective-permute-start.27 = (bf16[32,4,1,128]{3,0,2,1:T(8,128)(2,1)S(1)}, bf16[32,4,1,128]{3,0,2,1:T(8,128)(2,1)S(1)}, u32[]{:S(2)}, u32[]{:S(2)}) collective-permute-start(bf16[32,4,1,128]{3,0,2,1:T(8,128)(2,1)S(1)} %get-tuple-element.609), channel_id=1, source_target_pairs={{0,1},{1,2},{2,3},{3,4},{4,5},{5,6},{6,7},{8,9},{9,10},{10,11},{11... | collective-permute-start | bytes 98312 | tf_op jit(solution)/shard_map/ppermute | solution.py:12
  186.1 1.7 collective-permute-start.28
  189.2 3.4 collective-permute-start.32
  195.8 3.6 %collective-permute-start.29 = (bf16[32,4,1,128]{3,0,2,1:T(8,128)(2,1)S(1)}, bf16[32,4,1,128]{3,0,2,1:T(8,128)(2,1)S(1)}, u32[]{:S(2)}, u32[]{:S(2)}) collective-permute-start(bf16[32,4,1,128]{3,0,2,1:T(8,128)(2,1)S(1)} %get-tuple-element.607), channel_id=1, source_target_pairs={{0,1},{1,2},{2,3},{3,4},{4,5},{5,6},{6,7},{8,9},{9,10},{10,11},{11... | collective-permute-start | bytes 98312 | tf_op jit(solution)/shard_map/ppermute | solution.py:12
  199.5 1.3 collective-permute-start.30
  202.1 1.9 collective-permute-done.30
  207.5 1.3 collective-permute-start.33
  208.9 6.9 %collective-permute-done.33 = bf16[32,4,4,128]{3,0,2,1:T(8,128)(2,1)S(1)} collective-permute-done((bf16[32,4,4,128]{3,0,2,1:T(8,128)(2,1)S(1)}, bf16[32,4,4,128]{3,0,2,1:T(8,128)(2,1)S(1)}, u32[]{:S(2)}, u32[]{:S(2)}) %collective-permute-start.33) | collective-permute-done | bytes 131104 | tf_op jit(solution)/shard_map/ppermute | solution.py:27
  216.0 2.8 collective-permute-start.34
  218.8 1.3 collective-permute-start.35
  226.1 4.8 %collective-permute-start.36 = (bf16[32,4,1,128]{3,0,2,1:T(8,128)(2,1)S(1)}, bf16[32,4,1,128]{3,0,2,1:T(8,128)(2,1)S(1)}, u32[]{:S(2)}, u32[]{:S(2)}) collective-permute-start(bf16[32,4,1,128]{3,0,2,1:T(8,128)(2,1)S(1)} %get-tuple-element.603), channel_id=1, source_target_pairs={{0,1},{1,2},{2,3},{3,4},{4,5},{5,6},{6,7},{8,9},{9,10},{10,11},{11... | collective-permute-start | bytes 98312 | tf_op jit(solution)/shard_map/ppermute | solution.py:12
  230.9 1.5 collective-permute-start.37
  237.4 1.9 collective-permute-start.45
  240.6 6.0 %collective-permute-done.40 = bf16[32,4,4,128]{3,0,2,1:T(8,128)(2,1)S(1)} collective-permute-done((bf16[32,4,4,128]{3,0,2,1:T(8,128)(2,1)S(1)}, bf16[32,4,4,128]{3,0,2,1:T(8,128)(2,1)S(1)}, u32[]{:S(2)}, u32[]{:S(2)}) %collective-permute-start.40) | collective-permute-done | bytes 131104 | tf_op jit(solution)/shard_map/ppermute | solution.py:27
  246.8 2.6 collective-permute-start.41
  249.4 1.3 collective-permute-start.42
  256.5 4.5 %collective-permute-start.43 = (bf16[32,4,1,128]{3,0,2,1:T(8,128)(2,1)S(1)}, bf16[32,4,1,128]{3,0,2,1:T(8,128)(2,1)S(1)}, u32[]{:S(2)}, u32[]{:S(2)}) collective-permute-start(bf16[32,4,1,128]{3,0,2,1:T(8,128)(2,1)S(1)} %get-tuple-element.599), channel_id=1, source_target_pairs={{0,1},{1,2},{2,3},{3,4},{4,5},{5,6},{6,7},{8,9},{9,10},{10,11},{11... | collective-permute-start | bytes 98312 | tf_op jit(solution)/shard_map/ppermute | solution.py:12
  261.0 1.3 collective-permute-start.44
  268.2 1.3 collective-permute-start.47
  269.5 2.7 collective-permute-start.52
  272.3 2.7 collective-permute-done.47
  275.2 4.6 %collective-permute-start.48 = (bf16[32,4,1,128]{3,0,2,1:T(8,128)(2,1)S(1)}, bf16[32,4,1,128]{3,0,2,1:T(8,128)(2,1)S(1)}, u32[]{:S(2)}, u32[]{:S(2)}) collective-permute-start(bf16[32,4,1,128]{3,0,2,1:T(8,128)(2,1)S(1)} %get-tuple-element.597), channel_id=1, source_target_pairs={{0,1},{1,2},{2,3},{3,4},{4,5},{5,6},{6,7},{8,9},{9,10},{10,11},{11... | collective-permute-start | bytes 98312 | tf_op jit(solution)/shard_map/ppermute | solution.py:12
  279.8 1.5 collective-permute-start.49
  287.0 4.8 %collective-permute-start.50 = (bf16[32,4,1,128]{3,0,2,1:T(8,128)(2,1)S(1)}, bf16[32,4,1,128]{3,0,2,1:T(8,128)(2,1)S(1)}, u32[]{:S(2)}, u32[]{:S(2)}) collective-permute-start(bf16[32,4,1,128]{3,0,2,1:T(8,128)(2,1)S(1)} %get-tuple-element.595), channel_id=1, source_target_pairs={{0,1},{1,2},{2,3},{3,4},{4,5},{5,6},{6,7},{8,9},{9,10},{10,11},{11... | collective-permute-start | bytes 98312 | tf_op jit(solution)/shard_map/ppermute | solution.py:12
  294.5 1.3 fusion.154
  299.0 52.9 %all-reduce.22.cloned.1.call-done = bf16[1,2,27,32,32]{4,3,2,1,0:T(8,128)(2,1)} async-done(((bf16[1,2,27,32,32]{4,3,2,1,0:T(8,128)(2,1)}), bf16[1,2,27,32,32]{4,3,2,1,0:T(8,128)(2,1)}) %all-reduce.22.cloned.1.call-update) | async-done | bytes 110608 | tf_op jit(solution)/shard_map/psum | solution.py:204
  351.9 2.0 broadcast_in_dim.214
  (761 shorter events, 122.3 us)
Async XLA Ops:
  7.2 7.5 %copy-start = (bf16[1,2,27,32,32]{4,3,2,1,0:T(8,128)(2,1)S(1)}, bf16[1,2,27,32,32]{4,3,2,1,0:T(8,128)(2,1)}, u32[]{:S(2)}) copy-start(bf16[1,2,27,32,32]{4,3,2,1,0:T(8,128)(2,1)} %param.5) | copy-start | bytes 331780
  7.2 344.7 %all-reduce.22.cloned.1.call-start = ((), (), s32[]{:S(2)}) async-start(), calls=%async_computation | async-start | bytes 884736 | tf_op jit(solution)/shard_map/psum | solution.py:204
  8.7 6.1 %copy-start.1 = (bf16[2,32,4,4,128]{4,3,2,1,0:T(4,128)(2,1)S(1)}, bf16[2,32,4,4,128]{4,3,2,1,0:T(4,128)(2,1)}, u32[]{:S(2)}) copy-start(bf16[2,32,4,4,128]{4,3,2,1,0:T(4,128)(2,1)} %param.4) | copy-start | bytes 786436
  8.7 20.7 %collective-permute-start.3 = (bf16[32,4,4,128]{3,0,2,1:T(8,128)(2,1)S(1)}, bf16[32,4,4,128]{3,0,2,1:T(8,128)(2,1)S(1)}, u32[]{:S(2)}, u32[]{:S(2)}) collective-permute-start(bf16[32,4,4,128]{3,0,2,1:T(8,128)(2,1)S(1)} %fusion.577), channel_id=1, source_target_pairs={{0,8},{8,0},{16,24},{24,16},{1,9},{9,1},{17,25},{25,17},{2,10},{10... | collective-permute-start | bytes 393224 | tf_op jit(solution)/shard_map/ppermute | solution.py:21
  11.8 3.3 collective-permute-start
  13.2 4.8 %collective-permute-start.1 = (bf16[32,4,2,128]{3,0,2,1:T(8,128)(2,1)S(1)}, bf16[32,4,2,128]{3,0,2,1:T(8,128)(2,1)S(1)}, u32[]{:S(2)}, u32[]{:S(2)}) collective-permute-start(bf16[32,4,2,128]{3,0,2,1:T(8,128)(2,1)S(1)} %get-tuple-element.624), channel_id=1, source_target_pairs={{1,0},{2,1},{3,2},{4,3},{5,4},{6,5},{7,6},{9,8},{10,9},{11,10},{12... | collective-permute-start | bytes 196616 | tf_op jit(solution)/shard_map/ppermute | solution.py:15
  26.1 10.4 %collective-permute-start.2 = (bf16[32,4,4,128]{3,0,2,1:T(8,128)(2,1)S(1)}, bf16[32,4,4,128]{3,0,2,1:T(8,128)(2,1)S(1)}, u32[]{:S(2)}, u32[]{:S(2)}) collective-permute-start(bf16[32,4,4,128]{3,0,2,1:T(8,128)(2,1)S(1)} %get-tuple-element.35), channel_id=1, source_target_pairs={{0,8},{8,16},{16,24},{1,9},{9,17},{17,25},{2,10},{10,18},{18,26},{... | collective-permute-start | bytes 393224 | tf_op jit(solution)/shard_map/ppermute | solution.py:27
  29.5 7.0 %collective-permute-start.4 = (bf16[32,4,4,128]{3,0,2,1:T(8,128)(2,1)S(1)}, bf16[32,4,4,128]{3,0,2,1:T(8,128)(2,1)S(1)}, u32[]{:S(2)}, u32[]{:S(2)}) collective-permute-start(bf16[32,4,4,128]{3,0,2,1:T(8,128)(2,1)S(1)} %collective-permute-done.3), channel_id=1, source_target_pairs={{0,16},{8,24},{16,0},{24,8},{1,17},{9,25},{17,1},{25,9},{2,18},{10... | collective-permute-start | bytes 393224 | tf_op jit(solution)/shard_map/ppermute | solution.py:21
  36.7 5.4 %collective-permute-start.5 = (bf16[32,4,2,128]{3,0,2,1:T(8,128)(2,1)S(1)}, bf16[32,4,2,128]{3,0,2,1:T(8,128)(2,1)S(1)}, u32[]{:S(2)}, u32[]{:S(2)}) collective-permute-start(bf16[32,4,2,128]{3,0,2,1:T(8,128)(2,1)S(1)} %get-tuple-element.621), channel_id=1, source_target_pairs={{0,1},{1,2},{2,3},{3,4},{4,5},{5,6},{6,7},{8,9},{9,10},{10,11},{11... | collective-permute-start | bytes 196616 | tf_op jit(solution)/shard_map/ppermute | solution.py:12
  39.4 5.4 %collective-permute-start.6 = (bf16[32,4,2,128]{3,0,2,1:T(8,128)(2,1)S(1)}, bf16[32,4,2,128]{3,0,2,1:T(8,128)(2,1)S(1)}, u32[]{:S(2)}, u32[]{:S(2)}) collective-permute-start(bf16[32,4,2,128]{3,0,2,1:T(8,128)(2,1)S(1)} %get-tuple-element.622), channel_id=1, source_target_pairs={{1,0},{2,1},{3,2},{4,3},{5,4},{6,5},{7,6},{9,8},{10,9},{11,10},{12... | collective-permute-start | bytes 196616 | tf_op jit(solution)/shard_map/ppermute | solution.py:15
  40.9 15.3 %collective-permute-start.8 = (bf16[32,4,4,128]{3,0,2,1:T(8,128)(2,1)S(1)}, bf16[32,4,4,128]{3,0,2,1:T(8,128)(2,1)S(1)}, u32[]{:S(2)}, u32[]{:S(2)}) collective-permute-start(bf16[32,4,4,128]{3,0,2,1:T(8,128)(2,1)S(1)} %get-tuple-element.33), channel_id=1, source_target_pairs={{0,8},{8,0},{16,24},{24,16},{1,9},{9,1},{17,25},{25,17},{2,10},{10... | collective-permute-start | bytes 393224 | tf_op jit(solution)/shard_map/ppermute | solution.py:21
  52.8 11.4 %collective-permute-start.7 = (bf16[32,4,4,128]{3,0,2,1:T(8,128)(2,1)S(1)}, bf16[32,4,4,128]{3,0,2,1:T(8,128)(2,1)S(1)}, u32[]{:S(2)}, u32[]{:S(2)}) collective-permute-start(bf16[32,4,4,128]{3,0,2,1:T(8,128)(2,1)S(1)} %get-tuple-element.29), channel_id=1, source_target_pairs={{0,8},{8,16},{16,24},{1,9},{9,17},{17,25},{2,10},{10,18},{18,26},{... | collective-permute-start | bytes 393224 | tf_op jit(solution)/shard_map/ppermute | solution.py:27
  56.2 7.9 %collective-permute-start.9 = (bf16[32,4,4,128]{3,0,2,1:T(8,128)(2,1)S(1)}, bf16[32,4,4,128]{3,0,2,1:T(8,128)(2,1)S(1)}, u32[]{:S(2)}, u32[]{:S(2)}) collective-permute-start(bf16[32,4,4,128]{3,0,2,1:T(8,128)(2,1)S(1)} %collective-permute-done.8), channel_id=1, source_target_pairs={{0,16},{8,24},{16,0},{24,8},{1,17},{9,25},{17,1},{25,9},{2,18},{10... | collective-permute-start | bytes 393224 | tf_op jit(solution)/shard_map/ppermute | solution.py:21
  64.3 5.1 %collective-permute-start.10 = (bf16[32,4,2,128]{3,0,2,1:T(8,128)(2,1)S(1)}, bf16[32,4,2,128]{3,0,2,1:T(8,128)(2,1)S(1)}, u32[]{:S(2)}, u32[]{:S(2)}) collective-permute-start(bf16[32,4,2,128]{3,0,2,1:T(8,128)(2,1)S(1)} %get-tuple-element.619), channel_id=1, source_target_pairs={{0,1},{1,2},{2,3},{3,4},{4,5},{5,6},{6,7},{8,9},{9,10},{10,11},{11... | collective-permute-start | bytes 196616 | tf_op jit(solution)/shard_map/ppermute | solution.py:12
  66.9 5.5 %collective-permute-start.11 = (bf16[32,4,2,128]{3,0,2,1:T(8,128)(2,1)S(1)}, bf16[32,4,2,128]{3,0,2,1:T(8,128)(2,1)S(1)}, u32[]{:S(2)}, u32[]{:S(2)}) collective-permute-start(bf16[32,4,2,128]{3,0,2,1:T(8,128)(2,1)S(1)} %get-tuple-element.620), channel_id=1, source_target_pairs={{1,0},{2,1},{3,2},{4,3},{5,4},{6,5},{7,6},{9,8},{10,9},{11,10},{12... | collective-permute-start | bytes 196616 | tf_op jit(solution)/shard_map/ppermute | solution.py:15
  68.2 15.8 %collective-permute-start.13 = (bf16[32,4,4,128]{3,0,2,1:T(8,128)(2,1)S(1)}, bf16[32,4,4,128]{3,0,2,1:T(8,128)(2,1)S(1)}, u32[]{:S(2)}, u32[]{:S(2)}) collective-permute-start(bf16[32,4,4,128]{3,0,2,1:T(8,128)(2,1)S(1)} %get-tuple-element.27), channel_id=1, source_target_pairs={{0,8},{8,0},{16,24},{24,16},{1,9},{9,1},{17,25},{25,17},{2,10},{10... | collective-permute-start | bytes 393224 | tf_op jit(solution)/shard_map/ppermute | solution.py:21
  80.5 11.4 %collective-permute-start.12 = (bf16[32,4,4,128]{3,0,2,1:T(8,128)(2,1)S(1)}, bf16[32,4,4,128]{3,0,2,1:T(8,128)(2,1)S(1)}, u32[]{:S(2)}, u32[]{:S(2)}) collective-permute-start(bf16[32,4,4,128]{3,0,2,1:T(8,128)(2,1)S(1)} %get-tuple-element.23), channel_id=1, source_target_pairs={{0,8},{8,16},{16,24},{1,9},{9,17},{17,25},{2,10},{10,18},{18,26},{... | collective-permute-start | bytes 393224 | tf_op jit(solution)/shard_map/ppermute | solution.py:27
  84.1 7.7 %collective-permute-start.14 = (bf16[32,4,4,128]{3,0,2,1:T(8,128)(2,1)S(1)}, bf16[32,4,4,128]{3,0,2,1:T(8,128)(2,1)S(1)}, u32[]{:S(2)}, u32[]{:S(2)}) collective-permute-start(bf16[32,4,4,128]{3,0,2,1:T(8,128)(2,1)S(1)} %collective-permute-done.13), channel_id=1, source_target_pairs={{0,16},{8,24},{16,0},{24,8},{1,17},{9,25},{17,1},{25,9},{2,18},{10... | collective-permute-start | bytes 393224 | tf_op jit(solution)/shard_map/ppermute | solution.py:21
  92.0 5.5 %collective-permute-start.15 = (bf16[32,4,2,128]{3,0,2,1:T(8,128)(2,1)S(1)}, bf16[32,4,2,128]{3,0,2,1:T(8,128)(2,1)S(1)}, u32[]{:S(2)}, u32[]{:S(2)}) collective-permute-start(bf16[32,4,2,128]{3,0,2,1:T(8,128)(2,1)S(1)} %get-tuple-element.617), channel_id=1, source_target_pairs={{0,1},{1,2},{2,3},{3,4},{4,5},{5,6},{6,7},{8,9},{9,10},{10,11},{11... | collective-permute-start | bytes 196616 | tf_op jit(solution)/shard_map/ppermute | solution.py:12
  94.7 5.3 %collective-permute-start.16 = (bf16[32,4,2,128]{3,0,2,1:T(8,128)(2,1)S(1)}, bf16[32,4,2,128]{3,0,2,1:T(8,128)(2,1)S(1)}, u32[]{:S(2)}, u32[]{:S(2)}) collective-permute-start(bf16[32,4,2,128]{3,0,2,1:T(8,128)(2,1)S(1)} %get-tuple-element.618), channel_id=1, source_target_pairs={{1,0},{2,1},{3,2},{4,3},{5,4},{6,5},{7,6},{9,8},{10,9},{11,10},{12... | collective-permute-start | bytes 196616 | tf_op jit(solution)/shard_map/ppermute | solution.py:15
  96.0 12.7 %collective-permute-start.18 = (bf16[32,4,4,128]{3,0,2,1:T(8,128)(2,1)S(1)}, bf16[32,4,4,128]{3,0,2,1:T(8,128)(2,1)S(1)}, u32[]{:S(2)}, u32[]{:S(2)}) collective-permute-start(bf16[32,4,4,128]{3,0,2,1:T(8,128)(2,1)S(1)} %get-tuple-element.21), channel_id=1, source_target_pairs={{0,8},{8,0},{16,24},{24,16},{1,9},{9,1},{17,25},{25,17},{2,10},{10... | collective-permute-start | bytes 393224 | tf_op jit(solution)/shard_map/ppermute | solution.py:21
  108.7 5.5 %collective-permute-start.19 = (bf16[32,4,4,128]{3,0,2,1:T(8,128)(2,1)S(1)}, bf16[32,4,4,128]{3,0,2,1:T(8,128)(2,1)S(1)}, u32[]{:S(2)}, u32[]{:S(2)}) collective-permute-start(bf16[32,4,4,128]{3,0,2,1:T(8,128)(2,1)S(1)} %collective-permute-done.18), channel_id=1, source_target_pairs={{0,16},{8,24},{16,0},{24,8},{1,17},{9,25},{17,1},{25,9},{2,18},{10... | collective-permute-start | bytes 393224 | tf_op jit(solution)/shard_map/ppermute | solution.py:21
  111.2 3.8 %collective-permute-start.17 = (bf16[32,4,4,128]{3,0,2,1:T(8,128)(2,1)S(1)}, bf16[32,4,4,128]{3,0,2,1:T(8,128)(2,1)S(1)}, u32[]{:S(2)}, u32[]{:S(2)}) collective-permute-start(bf16[32,4,4,128]{3,0,2,1:T(8,128)(2,1)S(1)} %get-tuple-element.17), channel_id=1, source_target_pairs={{0,8},{8,16},{16,24},{1,9},{9,17},{17,25},{2,10},{10,18},{18,26},{... | collective-permute-start | bytes 393224 | tf_op jit(solution)/shard_map/ppermute | solution.py:27
  115.1 5.5 %collective-permute-start.20 = (bf16[32,4,2,128]{3,0,2,1:T(8,128)(2,1)S(1)}, bf16[32,4,2,128]{3,0,2,1:T(8,128)(2,1)S(1)}, u32[]{:S(2)}, u32[]{:S(2)}) collective-permute-start(bf16[32,4,2,128]{3,0,2,1:T(8,128)(2,1)S(1)} %get-tuple-element.615), channel_id=1, source_target_pairs={{0,1},{1,2},{2,3},{3,4},{4,5},{5,6},{6,7},{8,9},{9,10},{10,11},{11... | collective-permute-start | bytes 196616 | tf_op jit(solution)/shard_map/ppermute | solution.py:12
  119.2 4.2 %collective-permute-start.21 = (bf16[32,4,2,128]{3,0,2,1:T(8,128)(2,1)S(1)}, bf16[32,4,2,128]{3,0,2,1:T(8,128)(2,1)S(1)}, u32[]{:S(2)}, u32[]{:S(2)}) collective-permute-start(bf16[32,4,2,128]{3,0,2,1:T(8,128)(2,1)S(1)} %get-tuple-element.616), channel_id=1, source_target_pairs={{1,0},{2,1},{3,2},{4,3},{5,4},{6,5},{7,6},{9,8},{10,9},{11,10},{12... | collective-permute-start | bytes 196616 | tf_op jit(solution)/shard_map/ppermute | solution.py:15
  131.4 29.1 %collective-permute-start.22 = (bf16[32,4,1,128]{3,0,2,1:T(8,128)(2,1)S(1)}, bf16[32,4,1,128]{3,0,2,1:T(8,128)(2,1)S(1)}, u32[]{:S(2)}, u32[]{:S(2)}) collective-permute-start(bf16[32,4,1,128]{3,0,2,1:T(8,128)(2,1)S(1)} %get-tuple-element.613), channel_id=1, source_target_pairs={{0,1},{1,2},{2,3},{3,4},{4,5},{5,6},{6,7},{8,9},{9,10},{10,11},{11... | collective-permute-start | bytes 98312 | tf_op jit(solution)/shard_map/ppermute | solution.py:12
  136.3 24.3 %collective-permute-start.23 = (bf16[32,4,1,128]{3,0,2,1:T(8,128)(2,1)S(1)}, bf16[32,4,1,128]{3,0,2,1:T(8,128)(2,1)S(1)}, u32[]{:S(2)}, u32[]{:S(2)}) collective-permute-start(bf16[32,4,1,128]{3,0,2,1:T(8,128)(2,1)S(1)} %get-tuple-element.614), channel_id=1, source_target_pairs={{1,0},{2,1},{3,2},{4,3},{5,4},{6,5},{7,6},{9,8},{10,9},{11,10},{12... | collective-permute-start | bytes 98312 | tf_op jit(solution)/shard_map/ppermute | solution.py:15
  164.0 5.7 %collective-permute-start.24 = (bf16[32,4,1,128]{3,0,2,1:T(8,128)(2,1)S(1)}, bf16[32,4,1,128]{3,0,2,1:T(8,128)(2,1)S(1)}, u32[]{:S(2)}, u32[]{:S(2)}) collective-permute-start(bf16[32,4,1,128]{3,0,2,1:T(8,128)(2,1)S(1)} %get-tuple-element.611), channel_id=1, source_target_pairs={{0,1},{1,2},{2,3},{3,4},{4,5},{5,6},{6,7},{8,9},{9,10},{10,11},{11... | collective-permute-start | bytes 98312 | tf_op jit(solution)/shard_map/ppermute | solution.py:12
  167.0 3.9 %collective-permute-start.25 = (bf16[32,4,1,128]{3,0,2,1:T(8,128)(2,1)S(1)}, bf16[32,4,1,128]{3,0,2,1:T(8,128)(2,1)S(1)}, u32[]{:S(2)}, u32[]{:S(2)}) collective-permute-start(bf16[32,4,1,128]{3,0,2,1:T(8,128)(2,1)S(1)} %get-tuple-element.612), channel_id=1, source_target_pairs={{1,0},{2,1},{3,2},{4,3},{5,4},{6,5},{7,6},{9,8},{10,9},{11,10},{12... | collective-permute-start | bytes 98312 | tf_op jit(solution)/shard_map/ppermute | solution.py:15
  174.1 7.3 %collective-permute-start.26 = (bf16[32,4,4,128]{3,0,2,1:T(8,128)(2,1)S(1)}, bf16[32,4,4,128]{3,0,2,1:T(8,128)(2,1)S(1)}, u32[]{:S(2)}, u32[]{:S(2)}) collective-permute-start(bf16[32,4,4,128]{3,0,2,1:T(8,128)(2,1)S(1)} %get-tuple-element.13), channel_id=1, source_target_pairs={{8,0},{16,8},{24,16},{9,1},{17,9},{25,17},{10,2},{18,10},{26,18},{... | collective-permute-start | bytes 393224 | tf_op jit(solution)/shard_map/ppermute | solution.py:27
  175.5 13.7 %collective-permute-start.31 = (bf16[32,4,4,128]{3,0,2,1:T(8,128)(2,1)S(1)}, bf16[32,4,4,128]{3,0,2,1:T(8,128)(2,1)S(1)}, u32[]{:S(2)}, u32[]{:S(2)}) collective-permute-start(bf16[32,4,4,128]{3,0,2,1:T(8,128)(2,1)S(1)} %get-tuple-element.13), channel_id=1, source_target_pairs={{0,8},{8,0},{16,24},{24,16},{1,9},{9,1},{17,25},{25,17},{2,10},{10... | collective-permute-start | bytes 393224 | tf_op jit(solution)/shard_map/ppermute | solution.py:21
  181.6 11.0 %collective-permute-start.27 = (bf16[32,4,1,128]{3,0,2,1:T(8,128)(2,1)S(1)}, bf16[32,4,1,128]{3,0,2,1:T(8,128)(2,1)S(1)}, u32[]{:S(2)}, u32[]{:S(2)}) collective-permute-start(bf16[32,4,1,128]{3,0,2,1:T(8,128)(2,1)S(1)} %get-tuple-element.609), channel_id=1, source_target_pairs={{0,1},{1,2},{2,3},{3,4},{4,5},{5,6},{6,7},{8,9},{9,10},{10,11},{11... | collective-permute-start | bytes 98312 | tf_op jit(solution)/shard_map/ppermute | solution.py:12
  186.1 6.5 %collective-permute-start.28 = (bf16[32,4,1,128]{3,0,2,1:T(8,128)(2,1)S(1)}, bf16[32,4,1,128]{3,0,2,1:T(8,128)(2,1)S(1)}, u32[]{:S(2)}, u32[]{:S(2)}) collective-permute-start(bf16[32,4,1,128]{3,0,2,1:T(8,128)(2,1)S(1)} %get-tuple-element.610), channel_id=1, source_target_pairs={{1,0},{2,1},{3,2},{4,3},{5,4},{6,5},{7,6},{9,8},{10,9},{11,10},{12... | collective-permute-start | bytes 98312 | tf_op jit(solution)/shard_map/ppermute | solution.py:15
  189.2 18.0 %collective-permute-start.32 = (bf16[32,4,4,128]{3,0,2,1:T(8,128)(2,1)S(1)}, bf16[32,4,4,128]{3,0,2,1:T(8,128)(2,1)S(1)}, u32[]{:S(2)}, u32[]{:S(2)}) collective-permute-start(bf16[32,4,4,128]{3,0,2,1:T(8,128)(2,1)S(1)} %collective-permute-done.31), channel_id=1, source_target_pairs={{0,16},{8,24},{16,0},{24,8},{1,17},{9,25},{17,1},{25,9},{2,18},{10... | collective-permute-start | bytes 393224 | tf_op jit(solution)/shard_map/ppermute | solution.py:21
  195.8 6.3 %collective-permute-start.29 = (bf16[32,4,1,128]{3,0,2,1:T(8,128)(2,1)S(1)}, bf16[32,4,1,128]{3,0,2,1:T(8,128)(2,1)S(1)}, u32[]{:S(2)}, u32[]{:S(2)}) collective-permute-start(bf16[32,4,1,128]{3,0,2,1:T(8,128)(2,1)S(1)} %get-tuple-element.607), channel_id=1, source_target_pairs={{0,1},{1,2},{2,3},{3,4},{4,5},{5,6},{6,7},{8,9},{9,10},{10,11},{11... | collective-permute-start | bytes 98312 | tf_op jit(solution)/shard_map/ppermute | solution.py:12
  199.5 4.6 %collective-permute-start.30 = (bf16[32,4,1,128]{3,0,2,1:T(8,128)(2,1)S(1)}, bf16[32,4,1,128]{3,0,2,1:T(8,128)(2,1)S(1)}, u32[]{:S(2)}, u32[]{:S(2)}) collective-permute-start(bf16[32,4,1,128]{3,0,2,1:T(8,128)(2,1)S(1)} %get-tuple-element.608), channel_id=1, source_target_pairs={{1,0},{2,1},{3,2},{4,3},{5,4},{6,5},{7,6},{9,8},{10,9},{11,10},{12... | collective-permute-start | bytes 98312 | tf_op jit(solution)/shard_map/ppermute | solution.py:15
  207.4 14.1 %collective-permute-start.38 = (bf16[32,4,4,128]{3,0,2,1:T(8,128)(2,1)S(1)}, bf16[32,4,4,128]{3,0,2,1:T(8,128)(2,1)S(1)}, u32[]{:S(2)}, u32[]{:S(2)}) collective-permute-start(bf16[32,4,4,128]{3,0,2,1:T(8,128)(2,1)S(1)} %get-tuple-element.11), channel_id=1, source_target_pairs={{0,8},{8,0},{16,24},{24,16},{1,9},{9,1},{17,25},{25,17},{2,10},{10... | collective-permute-start | bytes 393224 | tf_op jit(solution)/shard_map/ppermute | solution.py:21
  207.5 8.3 %collective-permute-start.33 = (bf16[32,4,4,128]{3,0,2,1:T(8,128)(2,1)S(1)}, bf16[32,4,4,128]{3,0,2,1:T(8,128)(2,1)S(1)}, u32[]{:S(2)}, u32[]{:S(2)}) collective-permute-start(bf16[32,4,4,128]{3,0,2,1:T(8,128)(2,1)S(1)} %fusion.277), channel_id=1, source_target_pairs={{8,0},{16,8},{24,16},{9,1},{17,9},{25,17},{10,2},{18,10},{26,18},{... | collective-permute-start | bytes 393224 | tf_op jit(solution)/shard_map/ppermute | solution.py:27
  216.0 6.2 %collective-permute-start.34 = (bf16[32,4,1,128]{3,0,2,1:T(8,128)(2,1)S(1)}, bf16[32,4,1,128]{3,0,2,1:T(8,128)(2,1)S(1)}, u32[]{:S(2)}, u32[]{:S(2)}) collective-permute-start(bf16[32,4,1,128]{3,0,2,1:T(8,128)(2,1)S(1)} %get-tuple-element.605), channel_id=1, source_target_pairs={{0,1},{1,2},{2,3},{3,4},{4,5},{5,6},{6,7},{8,9},{9,10},{10,11},{11... | collective-permute-start | bytes 98312 | tf_op jit(solution)/shard_map/ppermute | solution.py:12
  218.8 4.0 %collective-permute-start.35 = (bf16[32,4,1,128]{3,0,2,1:T(8,128)(2,1)S(1)}, bf16[32,4,1,128]{3,0,2,1:T(8,128)(2,1)S(1)}, u32[]{:S(2)}, u32[]{:S(2)}) collective-permute-start(bf16[32,4,1,128]{3,0,2,1:T(8,128)(2,1)S(1)} %get-tuple-element.606), channel_id=1, source_target_pairs={{1,0},{2,1},{3,2},{4,3},{5,4},{6,5},{7,6},{9,8},{10,9},{11,10},{12... | collective-permute-start | bytes 98312 | tf_op jit(solution)/shard_map/ppermute | solution.py:15
  221.5 15.6 %collective-permute-start.39 = (bf16[32,4,4,128]{3,0,2,1:T(8,128)(2,1)S(1)}, bf16[32,4,4,128]{3,0,2,1:T(8,128)(2,1)S(1)}, u32[]{:S(2)}, u32[]{:S(2)}) collective-permute-start(bf16[32,4,4,128]{3,0,2,1:T(8,128)(2,1)S(1)} %collective-permute-done.38), channel_id=1, source_target_pairs={{0,16},{8,24},{16,0},{24,8},{1,17},{9,25},{17,1},{25,9},{2,18},{10... | collective-permute-start | bytes 393224 | tf_op jit(solution)/shard_map/ppermute | solution.py:21
  226.1 7.7 %collective-permute-start.36 = (bf16[32,4,1,128]{3,0,2,1:T(8,128)(2,1)S(1)}, bf16[32,4,1,128]{3,0,2,1:T(8,128)(2,1)S(1)}, u32[]{:S(2)}, u32[]{:S(2)}) collective-permute-start(bf16[32,4,1,128]{3,0,2,1:T(8,128)(2,1)S(1)} %get-tuple-element.603), channel_id=1, source_target_pairs={{0,1},{1,2},{2,3},{3,4},{4,5},{5,6},{6,7},{8,9},{9,10},{10,11},{11... | collective-permute-start | bytes 98312 | tf_op jit(solution)/shard_map/ppermute | solution.py:12
  230.9 3.1 collective-permute-start.37
  237.4 14.7 %collective-permute-start.45 = (bf16[32,4,4,128]{3,0,2,1:T(8,128)(2,1)S(1)}, bf16[32,4,4,128]{3,0,2,1:T(8,128)(2,1)S(1)}, u32[]{:S(2)}, u32[]{:S(2)}) collective-permute-start(bf16[32,4,4,128]{3,0,2,1:T(8,128)(2,1)S(1)} %get-tuple-element.9), channel_id=1, source_target_pairs={{0,8},{8,0},{16,24},{24,16},{1,9},{9,1},{17,25},{25,17},{2,10},{10... | collective-permute-start | bytes 393224 | tf_op jit(solution)/shard_map/ppermute | solution.py:21
  239.3 7.3 %collective-permute-start.40 = (bf16[32,4,4,128]{3,0,2,1:T(8,128)(2,1)S(1)}, bf16[32,4,4,128]{3,0,2,1:T(8,128)(2,1)S(1)}, u32[]{:S(2)}, u32[]{:S(2)}) collective-permute-start(bf16[32,4,4,128]{3,0,2,1:T(8,128)(2,1)S(1)} %fusion.276), channel_id=1, source_target_pairs={{8,0},{16,8},{24,16},{9,1},{17,9},{25,17},{10,2},{18,10},{26,18},{... | collective-permute-start | bytes 393224 | tf_op jit(solution)/shard_map/ppermute | solution.py:27
  246.8 6.5 %collective-permute-start.41 = (bf16[32,4,1,128]{3,0,2,1:T(8,128)(2,1)S(1)}, bf16[32,4,1,128]{3,0,2,1:T(8,128)(2,1)S(1)}, u32[]{:S(2)}, u32[]{:S(2)}) collective-permute-start(bf16[32,4,1,128]{3,0,2,1:T(8,128)(2,1)S(1)} %get-tuple-element.601), channel_id=1, source_target_pairs={{0,1},{1,2},{2,3},{3,4},{4,5},{5,6},{6,7},{8,9},{9,10},{10,11},{11... | collective-permute-start | bytes 98312 | tf_op jit(solution)/shard_map/ppermute | solution.py:12
  249.4 3.9 %collective-permute-start.42 = (bf16[32,4,1,128]{3,0,2,1:T(8,128)(2,1)S(1)}, bf16[32,4,1,128]{3,0,2,1:T(8,128)(2,1)S(1)}, u32[]{:S(2)}, u32[]{:S(2)}) collective-permute-start(bf16[32,4,1,128]{3,0,2,1:T(8,128)(2,1)S(1)} %get-tuple-element.602), channel_id=1, source_target_pairs={{1,0},{2,1},{3,2},{4,3},{5,4},{6,5},{7,6},{9,8},{10,9},{11,10},{12... | collective-permute-start | bytes 98312 | tf_op jit(solution)/shard_map/ppermute | solution.py:15
  252.1 15.8 %collective-permute-start.46 = (bf16[32,4,4,128]{3,0,2,1:T(8,128)(2,1)S(1)}, bf16[32,4,4,128]{3,0,2,1:T(8,128)(2,1)S(1)}, u32[]{:S(2)}, u32[]{:S(2)}) collective-permute-start(bf16[32,4,4,128]{3,0,2,1:T(8,128)(2,1)S(1)} %collective-permute-done.45), channel_id=1, source_target_pairs={{0,16},{8,24},{16,0},{24,8},{1,17},{9,25},{17,1},{25,9},{2,18},{10... | collective-permute-start | bytes 393224 | tf_op jit(solution)/shard_map/ppermute | solution.py:21
  256.5 7.2 %collective-permute-start.43 = (bf16[32,4,1,128]{3,0,2,1:T(8,128)(2,1)S(1)}, bf16[32,4,1,128]{3,0,2,1:T(8,128)(2,1)S(1)}, u32[]{:S(2)}, u32[]{:S(2)}) collective-permute-start(bf16[32,4,1,128]{3,0,2,1:T(8,128)(2,1)S(1)} %get-tuple-element.599), channel_id=1, source_target_pairs={{0,1},{1,2},{2,3},{3,4},{4,5},{5,6},{6,7},{8,9},{9,10},{10,11},{11... | collective-permute-start | bytes 98312 | tf_op jit(solution)/shard_map/ppermute | solution.py:12
  261.0 3.8 %collective-permute-start.44 = (bf16[32,4,1,128]{3,0,2,1:T(8,128)(2,1)S(1)}, bf16[32,4,1,128]{3,0,2,1:T(8,128)(2,1)S(1)}, u32[]{:S(2)}, u32[]{:S(2)}) collective-permute-start(bf16[32,4,1,128]{3,0,2,1:T(8,128)(2,1)S(1)} %get-tuple-element.600), channel_id=1, source_target_pairs={{1,0},{2,1},{3,2},{4,3},{5,4},{6,5},{7,6},{9,8},{10,9},{11,10},{12... | collective-permute-start | bytes 98312 | tf_op jit(solution)/shard_map/ppermute | solution.py:15
  268.2 6.9 %collective-permute-start.47 = (bf16[32,4,4,128]{3,0,2,1:T(8,128)(2,1)S(1)}, bf16[32,4,4,128]{3,0,2,1:T(8,128)(2,1)S(1)}, u32[]{:S(2)}, u32[]{:S(2)}) collective-permute-start(bf16[32,4,4,128]{3,0,2,1:T(8,128)(2,1)S(1)} %fusion.275), channel_id=1, source_target_pairs={{8,0},{16,8},{24,16},{9,1},{17,9},{25,17},{10,2},{18,10},{26,18},{... | collective-permute-start | bytes 393224 | tf_op jit(solution)/shard_map/ppermute | solution.py:27
  269.5 13.1 %collective-permute-start.52 = (bf16[32,4,4,128]{3,0,2,1:T(8,128)(2,1)S(1)}, bf16[32,4,4,128]{3,0,2,1:T(8,128)(2,1)S(1)}, u32[]{:S(2)}, u32[]{:S(2)}) collective-permute-start(bf16[32,4,4,128]{3,0,2,1:T(8,128)(2,1)S(1)} %get-tuple-element.7), channel_id=1, source_target_pairs={{0,8},{8,0},{16,24},{24,16},{1,9},{9,1},{17,25},{25,17},{2,10},{10... | collective-permute-start | bytes 393224 | tf_op jit(solution)/shard_map/ppermute | solution.py:21
  275.2 8.1 %collective-permute-start.48 = (bf16[32,4,1,128]{3,0,2,1:T(8,128)(2,1)S(1)}, bf16[32,4,1,128]{3,0,2,1:T(8,128)(2,1)S(1)}, u32[]{:S(2)}, u32[]{:S(2)}) collective-permute-start(bf16[32,4,1,128]{3,0,2,1:T(8,128)(2,1)S(1)} %get-tuple-element.597), channel_id=1, source_target_pairs={{0,1},{1,2},{2,3},{3,4},{4,5},{5,6},{6,7},{8,9},{9,10},{10,11},{11... | collective-permute-start | bytes 98312 | tf_op jit(solution)/shard_map/ppermute | solution.py:12
  279.8 4.0 %collective-permute-start.49 = (bf16[32,4,1,128]{3,0,2,1:T(8,128)(2,1)S(1)}, bf16[32,4,1,128]{3,0,2,1:T(8,128)(2,1)S(1)}, u32[]{:S(2)}, u32[]{:S(2)}) collective-permute-start(bf16[32,4,1,128]{3,0,2,1:T(8,128)(2,1)S(1)} %get-tuple-element.598), channel_id=1, source_target_pairs={{1,0},{2,1},{3,2},{4,3},{5,4},{6,5},{7,6},{9,8},{10,9},{11,10},{12... | collective-permute-start | bytes 98312 | tf_op jit(solution)/shard_map/ppermute | solution.py:15
  282.7 71.2 %collective-permute-start.53 = (bf16[32,4,4,128]{3,0,2,1:T(8,128)(2,1)S(1)}, bf16[32,4,4,128]{3,0,2,1:T(8,128)(2,1)S(1)}, u32[]{:S(2)}, u32[]{:S(2)}) collective-permute-start(bf16[32,4,4,128]{3,0,2,1:T(8,128)(2,1)S(1)} %collective-permute-done.52), channel_id=1, source_target_pairs={{0,16},{8,24},{16,0},{24,8},{1,17},{9,25},{17,1},{25,9},{2,18},{10... | collective-permute-start | bytes 393224 | tf_op jit(solution)/shard_map/ppermute | solution.py:21
  287.0 8.9 %collective-permute-start.50 = (bf16[32,4,1,128]{3,0,2,1:T(8,128)(2,1)S(1)}, bf16[32,4,1,128]{3,0,2,1:T(8,128)(2,1)S(1)}, u32[]{:S(2)}, u32[]{:S(2)}) collective-permute-start(bf16[32,4,1,128]{3,0,2,1:T(8,128)(2,1)S(1)} %get-tuple-element.595), channel_id=1, source_target_pairs={{0,1},{1,2},{2,3},{3,4},{4,5},{5,6},{6,7},{8,9},{9,10},{10,11},{11... | collective-permute-start | bytes 98312 | tf_op jit(solution)/shard_map/ppermute | solution.py:12
  291.8 4.0 %collective-permute-start.51 = (bf16[32,4,1,128]{3,0,2,1:T(8,128)(2,1)S(1)}, bf16[32,4,1,128]{3,0,2,1:T(8,128)(2,1)S(1)}, u32[]{:S(2)}, u32[]{:S(2)}) collective-permute-start(bf16[32,4,1,128]{3,0,2,1:T(8,128)(2,1)S(1)} %get-tuple-element.596), channel_id=1, source_target_pairs={{1,0},{2,1},{3,2},{4,3},{5,4},{6,5},{7,6},{9,8},{10,9},{11,10},{12... | collective-permute-start | bytes 98312 | tf_op jit(solution)/shard_map/ppermute | solution.py:15
Sparse Core Ops, SparseCore 0:
  296.0 55.8 all-reduce.21
where the time goes:
time: 369 us; the launch traced here: 362 us
  starting transfers between devices  117 us (32%)
  waiting for transfers between devices  111 us (30%)
  local copies, waits for them, and re-layouts  63.7 us (17%)
  matrix products  36.7 us (10%)
  between operations  19.6 us (5%)
  other arithmetic  14.5 us (4%)
    ppermute x15, starting transfers between devices, extended(): lax.ppermute(lax.slice_in_dim(block, block.shape[dim] - width, None, axis...  53.8 us
    psum x1, waiting for transfers between devices, local(): lax.psum(grad_sum.astype(jnp.bfloat16), 'gy').astype(jnp.float32)  52.9 us
    unnamed x379, local copies, waits for them, and re-layouts  47.9 us
    ppermute x16, starting transfers between devices, from_partner(): lax.ppermute(array, axis, [(i, i ^ 1 << bit) for i in range(lax.axis_size...  28.4 us
    dot_general x60, matrix products, convolve(): jnp.einsum('tczyx,tco->ozyx', slices_of(padded, plane_shift, row_count),...  23.6 us
    ppermute x15, starting transfers between devices, extended(): lax.ppermute(lax.slice_in_dim(block, 0, width, axis=dim), axis, backward)  20.5 us
    ppermute x15, waiting for transfers between devices, extended(): lax.ppermute(lax.slice_in_dim(block, 0, width, axis=dim), axis, backward)  19.7 us
    ppermute x8, waiting for transfers between devices, passed_along(): lax.ppermute(value, axis, [(source, source + steps) for source in range(f...  19.3 us
  transfers between devices with their start and end apart: 55, of which 21 were waited for; matrix products, arithmetic and copies ran while one was open for 27% of the time, Pallas kernels for 0%

commit v1 on v0

--- a/solution.py
+++ b/solution.py
@@ -201,7 +201,9 @@
                 arrived,
             )
             from_after = passed_along(passing, "segment", -1)
-    weight_grads = lax.psum(grad_sum.astype(jnp.bfloat16), "gy").astype(jnp.float32)
+    weight_grads = jnp.sum(lax.all_gather(grad_sum.astype(jnp.bfloat16), "gy"), axis=0).astype(
+        jnp.float32
+    )
     return (feature_store[None], weight_grads[None], input_grads[None])
 
 

time: 369 us -> 342 us (0.927)
  waiting for transfers between devices: 111 us -> 56.3 us
  blocking collectives: 0 us -> 34.1 us
  between operations: 19.6 us -> 6.22 us
    psum x1 -> x0, waiting for transfers between devices: 52.9 us -> none  [local(): lax.psum(grad_sum.astype(jnp.bfloat16), 'gy').astype(jnp.float32)]
    all_gather x0 -> x1, blocking collectives: none -> 34.1 us  [local(): lax.all_gather(grad_sum.astype(jnp.bfloat16), 'gy')]
    unnamed x379 -> x399, local copies, waits for them, and re-layouts: 47.9 us -> 49.9 us
  transfers between devices with their start and end apart: 55 -> 54, of which waited for: 21 -> 20; matrix products, arithmetic and copies ran while one was open for 27% -> 31% of each run, Pallas kernels for 0% -> 0%
where the time goes in v1:
time: 342 us; the launch traced here: 336 us
  starting transfers between devices  117 us (34%)
  local copies, waits for them, and re-layouts  67.1 us (20%)
  waiting for transfers between devices  56.3 us (16%)
  matrix products  36.7 us (11%)
  blocking collectives  34.1 us (10%)
  other arithmetic  17.8 us (5%)
  between operations  6.22 us (2%)
    ppermute x15, starting transfers between devices, extended(): lax.ppermute(lax.slice_in_dim(block, block.shape[dim] - width, None, axis...  54.2 us
    unnamed x399, local copies, waits for them, and re-layouts  49.9 us
    all_gather x1, blocking collectives, local(): lax.all_gather(grad_sum.astype(jnp.bfloat16), 'gy')  34.1 us
    ppermute x16, starting transfers between devices, from_partner(): lax.ppermute(array, axis, [(i, i ^ 1 << bit) for i in range(lax.axis_size...  28.3 us
    dot_general x60, matrix products, convolve(): jnp.einsum('tczyx,tco->ozyx', slices_of(padded, plane_shift, row_count),...  23.6 us
    ppermute x15, starting transfers between devices, extended(): lax.ppermute(lax.slice_in_dim(block, 0, width, axis=dim), axis, backward)  20.5 us
    ppermute x15, waiting for transfers between devices, extended(): lax.ppermute(lax.slice_in_dim(block, 0, width, axis=dim), axis, backward)  19.7 us
    ppermute x16, waiting for transfers between devices, from_partner(): lax.ppermute(array, axis, [(i, i ^ 1 << bit) for i in range(lax.axis_size...  18.7 us
  transfers between devices with their start and end apart: 54, of which 20 were waited for; matrix products, arithmetic and copies ran while one was open for 31% of the time, Pallas kernels for 0%

profile of v1, /device:TPU:0, one launch (start us, length us, event | category | flops | bytes accessed | tf_op | source)
XLA Modules:
  0.0 335.6 jit_solution(7008391962231899585)
XLA Ops:
  0.7 1.4 constant_dynamic-slice_fusion.38
  2.2 3.0 collective-permute-start.3
  5.2 1.5 collective-permute-start
  6.7 1.3 collective-permute-start.1
  8.5 3.0 collective-permute-done.1
  19.5 2.4 collective-permute-start.2
  22.9 1.6 collective-permute-start.4
  24.5 5.4 %collective-permute-done.4 = bf16[32,4,4,128]{3,0,2,1:T(8,128)(2,1)S(1)} collective-permute-done((bf16[32,4,4,128]{3,0,2,1:T(8,128)(2,1)S(1)}, bf16[32,4,4,128]{3,0,2,1:T(8,128)(2,1)S(1)}, u32[]{:S(2)}, u32[]{:S(2)}) %collective-permute-start.4) | collective-permute-done | bytes 131104 | tf_op jit(solution)/shard_map/ppermute | solution.py:21
  30.1 2.7 collective-permute-start.5
  32.8 1.5 collective-permute-start.6
  35.6 2.6 collective-permute-done.6
  46.2 2.7 collective-permute-start.7
  49.6 1.8 collective-permute-start.9
  51.5 6.1 %collective-permute-done.9 = bf16[32,4,4,128]{3,0,2,1:T(8,128)(2,1)S(1)} collective-permute-done((bf16[32,4,4,128]{3,0,2,1:T(8,128)(2,1)S(1)}, bf16[32,4,4,128]{3,0,2,1:T(8,128)(2,1)S(1)}, u32[]{:S(2)}, u32[]{:S(2)}) %collective-permute-start.9) | collective-permute-done | bytes 131104 | tf_op jit(solution)/shard_map/ppermute | solution.py:21
  57.7 2.6 collective-permute-start.10
  60.3 1.3 collective-permute-start.11
  62.8 3.0 collective-permute-done.11
  73.8 2.9 collective-permute-start.12
  77.4 2.0 collective-permute-start.14
  79.5 5.7 %collective-permute-done.14 = bf16[32,4,4,128]{3,0,2,1:T(8,128)(2,1)S(1)} collective-permute-done((bf16[32,4,4,128]{3,0,2,1:T(8,128)(2,1)S(1)}, bf16[32,4,4,128]{3,0,2,1:T(8,128)(2,1)S(1)}, u32[]{:S(2)}, u32[]{:S(2)}) %collective-permute-start.14) | collective-permute-done | bytes 131104 | tf_op jit(solution)/shard_map/ppermute | solution.py:21
  85.3 2.7 collective-permute-start.15
  88.0 1.3 collective-permute-start.16
  89.3 1.5 collective-permute-start.18
  90.8 2.6 collective-permute-done.16
  102.0 2.5 collective-permute-start.19
  104.6 1.3 collective-permute-start.17
  106.0 1.5 collective-permute-done.19
  108.5 4.1 %collective-permute-start.20 = (bf16[32,4,2,128]{3,0,2,1:T(8,128)(2,1)S(1)}, bf16[32,4,2,128]{3,0,2,1:T(8,128)(2,1)S(1)}, u32[]{:S(2)}, u32[]{:S(2)}) collective-permute-start(bf16[32,4,2,128]{3,0,2,1:T(8,128)(2,1)S(1)} %get-tuple-element.618), channel_id=1, source_target_pairs={{0,1},{1,2},{2,3},{3,4},{4,5},{5,6},{6,7},{8,9},{9,10},{10,11},{11... | collective-permute-start | bytes 196616 | tf_op jit(solution)/shard_map/ppermute | solution.py:12
  112.6 1.3 collective-permute-start.21
  114.0 2.8 collective-permute-done.21
  124.8 4.8 %collective-permute-start.22 = (bf16[32,4,1,128]{3,0,2,1:T(8,128)(2,1)S(1)}, bf16[32,4,1,128]{3,0,2,1:T(8,128)(2,1)S(1)}, u32[]{:S(2)}, u32[]{:S(2)}) collective-permute-start(bf16[32,4,1,128]{3,0,2,1:T(8,128)(2,1)S(1)} %get-tuple-element.616), channel_id=1, source_target_pairs={{0,1},{1,2},{2,3},{3,4},{4,5},{5,6},{6,7},{8,9},{9,10},{10,11},{11... | collective-permute-start | bytes 98312 | tf_op jit(solution)/shard_map/ppermute | solution.py:12
  129.6 1.5 collective-permute-start.23
  157.5 3.0 collective-permute-start.24
  160.6 1.3 collective-permute-start.25
  167.7 1.3 collective-permute-start.26
  169.0 3.1 collective-permute-start.31
  172.2 2.8 collective-permute-done.26
  175.1 4.5 %collective-permute-start.27 = (bf16[32,4,1,128]{3,0,2,1:T(8,128)(2,1)S(1)}, bf16[32,4,1,128]{3,0,2,1:T(8,128)(2,1)S(1)}, u32[]{:S(2)}, u32[]{:S(2)}) collective-permute-start(bf16[32,4,1,128]{3,0,2,1:T(8,128)(2,1)S(1)} %get-tuple-element.612), channel_id=1, source_target_pairs={{0,1},{1,2},{2,3},{3,4},{4,5},{5,6},{6,7},{8,9},{9,10},{10,11},{11... | collective-permute-start | bytes 98312 | tf_op jit(solution)/shard_map/ppermute | solution.py:12
  179.7 1.7 collective-permute-start.28
  182.8 3.4 %collective-permute-start.32 = (bf16[32,4,4,128]{3,0,2,1:T(8,128)(2,1)S(1)}, bf16[32,4,4,128]{3,0,2,1:T(8,128)(2,1)S(1)}, u32[]{:S(2)}, u32[]{:S(2)}) collective-permute-start(bf16[32,4,4,128]{3,0,2,1:T(8,128)(2,1)S(1)} %collective-permute-done.31), channel_id=1, source_target_pairs={{0,16},{8,24},{16,0},{24,8},{1,17},{9,25},{17,1},{25,9},{2,18},{10... | collective-permute-start | bytes 393224 | tf_op jit(solution)/shard_map/ppermute | solution.py:21
  189.5 3.6 %collective-permute-start.29 = (bf16[32,4,1,128]{3,0,2,1:T(8,128)(2,1)S(1)}, bf16[32,4,1,128]{3,0,2,1:T(8,128)(2,1)S(1)}, u32[]{:S(2)}, u32[]{:S(2)}) collective-permute-start(bf16[32,4,1,128]{3,0,2,1:T(8,128)(2,1)S(1)} %get-tuple-element.610), channel_id=1, source_target_pairs={{0,1},{1,2},{2,3},{3,4},{4,5},{5,6},{6,7},{8,9},{9,10},{10,11},{11... | collective-permute-start | bytes 98312 | tf_op jit(solution)/shard_map/ppermute | solution.py:12
  193.1 1.3 collective-permute-start.30
  195.8 1.9 collective-permute-done.30
  201.2 1.3 collective-permute-start.33
  202.6 6.9 %collective-permute-done.33 = bf16[32,4,4,128]{3,0,2,1:T(8,128)(2,1)S(1)} collective-permute-done((bf16[32,4,4,128]{3,0,2,1:T(8,128)(2,1)S(1)}, bf16[32,4,4,128]{3,0,2,1:T(8,128)(2,1)S(1)}, u32[]{:S(2)}, u32[]{:S(2)}) %collective-permute-start.33) | collective-permute-done | bytes 131104 | tf_op jit(solution)/shard_map/ppermute | solution.py:27
  209.7 2.8 collective-permute-start.34
  212.5 1.3 collective-permute-start.35
  219.8 4.8 %collective-permute-start.36 = (bf16[32,4,1,128]{3,0,2,1:T(8,128)(2,1)S(1)}, bf16[32,4,1,128]{3,0,2,1:T(8,128)(2,1)S(1)}, u32[]{:S(2)}, u32[]{:S(2)}) collective-permute-start(bf16[32,4,1,128]{3,0,2,1:T(8,128)(2,1)S(1)} %get-tuple-element.606), channel_id=1, source_target_pairs={{0,1},{1,2},{2,3},{3,4},{4,5},{5,6},{6,7},{8,9},{9,10},{10,11},{11... | collective-permute-start | bytes 98312 | tf_op jit(solution)/shard_map/ppermute | solution.py:12
  224.7 1.5 collective-permute-start.37
  231.1 1.9 collective-permute-start.45
  234.3 6.0 %collective-permute-done.40 = bf16[32,4,4,128]{3,0,2,1:T(8,128)(2,1)S(1)} collective-permute-done((bf16[32,4,4,128]{3,0,2,1:T(8,128)(2,1)S(1)}, bf16[32,4,4,128]{3,0,2,1:T(8,128)(2,1)S(1)}, u32[]{:S(2)}, u32[]{:S(2)}) %collective-permute-start.40) | collective-permute-done | bytes 131104 | tf_op jit(solution)/shard_map/ppermute | solution.py:27
  240.5 2.6 collective-permute-start.41
  243.1 1.3 collective-permute-start.42
  250.3 4.5 %collective-permute-start.43 = (bf16[32,4,1,128]{3,0,2,1:T(8,128)(2,1)S(1)}, bf16[32,4,1,128]{3,0,2,1:T(8,128)(2,1)S(1)}, u32[]{:S(2)}, u32[]{:S(2)}) collective-permute-start(bf16[32,4,1,128]{3,0,2,1:T(8,128)(2,1)S(1)} %get-tuple-element.602), channel_id=1, source_target_pairs={{0,1},{1,2},{2,3},{3,4},{4,5},{5,6},{6,7},{8,9},{9,10},{10,11},{11... | collective-permute-start | bytes 98312 | tf_op jit(solution)/shard_map/ppermute | solution.py:12
  254.8 1.3 collective-permute-start.44
  261.9 1.3 collective-permute-start.47
  263.3 2.7 collective-permute-start.52
  267.5 1.4 collective-permute-done.47
  269.0 4.7 %collective-permute-start.48 = (bf16[32,4,1,128]{3,0,2,1:T(8,128)(2,1)S(1)}, bf16[32,4,1,128]{3,0,2,1:T(8,128)(2,1)S(1)}, u32[]{:S(2)}, u32[]{:S(2)}) collective-permute-start(bf16[32,4,1,128]{3,0,2,1:T(8,128)(2,1)S(1)} %get-tuple-element.600), channel_id=1, source_target_pairs={{0,1},{1,2},{2,3},{3,4},{4,5},{5,6},{6,7},{8,9},{9,10},{10,11},{11... | collective-permute-start | bytes 98312 | tf_op jit(solution)/shard_map/ppermute | solution.py:12
  273.6 1.5 collective-permute-start.49
  281.5 5.1 %collective-permute-start.50 = (bf16[32,4,1,128]{3,0,2,1:T(8,128)(2,1)}, bf16[32,4,1,128]{3,0,2,1:T(8,128)(2,1)}, u32[]{:S(2)}, u32[]{:S(2)}) collective-permute-start(bf16[32,4,1,128]{3,0,2,1:T(8,128)(2,1)} %get-tuple-element.598), channel_id=1, source_target_pairs={{0,1},{1,2},{2,3},{3,4},{4,5},{5,6},{6,7},{8,9},{9,10},{10,11},{11... | collective-permute-start | bytes 98312 | tf_op jit(solution)/shard_map/ppermute | solution.py:12
  289.8 34.1 %all_gather.4 = bf16[8,2,27,32,32]{4,3,2,1,0:T(8,128)(2,1)S(1)} all-gather(bf16[1,2,27,32,32]{4,3,2,1,0:T(8,128)(2,1)S(1)} %fusion.128), channel_id=1, replica_groups=mesh['segment'=4,'gy'=8] {'gy'}, dimensions={0}, use_global_device_ids=true | all-gather | bytes 995328 | tf_op jit(solution)/shard_map/all_gather | solution.py:204
  324.0 1.7 reduce_sum.12
  325.7 2.1 bitcast_convert_fusion
  (780 shorter events, 128.4 us)
Async XLA Ops:
  0.6 7.4 %copy-start = (bf16[1,2,27,32,32]{4,3,2,1,0:T(8,128)(2,1)S(1)}, bf16[1,2,27,32,32]{4,3,2,1,0:T(8,128)(2,1)}, u32[]{:S(2)}) copy-start(bf16[1,2,27,32,32]{4,3,2,1,0:T(8,128)(2,1)} %param.5) | copy-start | bytes 331780
  2.1 6.1 %copy-start.8 = (bf16[2,32,4,4,128]{4,3,2,1,0:T(4,128)(2,1)S(1)}, bf16[2,32,4,4,128]{4,3,2,1,0:T(4,128)(2,1)}, u32[]{:S(2)}) copy-start(bf16[2,32,4,4,128]{4,3,2,1,0:T(4,128)(2,1)} %param.4) | copy-start | bytes 786436
  2.2 20.7 %collective-permute-start.3 = (bf16[32,4,4,128]{3,0,2,1:T(8,128)(2,1)S(1)}, bf16[32,4,4,128]{3,0,2,1:T(8,128)(2,1)S(1)}, u32[]{:S(2)}, u32[]{:S(2)}) collective-permute-start(bf16[32,4,4,128]{3,0,2,1:T(8,128)(2,1)S(1)} %fusion.576), channel_id=1, source_target_pairs={{0,8},{8,0},{16,24},{24,16},{1,9},{9,1},{17,25},{25,17},{2,10},{10... | collective-permute-start | bytes 393224 | tf_op jit(solution)/shard_map/ppermute | solution.py:21
  5.2 3.3 collective-permute-start
  6.7 4.8 %collective-permute-start.1 = (bf16[32,4,2,128]{3,0,2,1:T(8,128)(2,1)S(1)}, bf16[32,4,2,128]{3,0,2,1:T(8,128)(2,1)S(1)}, u32[]{:S(2)}, u32[]{:S(2)}) collective-permute-start(bf16[32,4,2,128]{3,0,2,1:T(8,128)(2,1)S(1)} %get-tuple-element.627), channel_id=1, source_target_pairs={{1,0},{2,1},{3,2},{4,3},{5,4},{6,5},{7,6},{9,8},{10,9},{11,10},{12... | collective-permute-start | bytes 196616 | tf_op jit(solution)/shard_map/ppermute | solution.py:15
  8.2 253.1 %copy-start.10 = (bf16[27,32,32]{1,2,0:T(8,128)(2,1)}, bf16[27,32,32]{1,2,0:T(8,128)(2,1)S(1)}, u32[]{:S(2)}) copy-start(bf16[27,32,32]{1,2,0:T(8,128)(2,1)S(1)} %reverse_bitcast_fusion) | copy-start | bytes 165892
  19.5 10.5 %collective-permute-start.2 = (bf16[32,4,4,128]{3,0,2,1:T(8,128)(2,1)S(1)}, bf16[32,4,4,128]{3,0,2,1:T(8,128)(2,1)S(1)}, u32[]{:S(2)}, u32[]{:S(2)}) collective-permute-start(bf16[32,4,4,128]{3,0,2,1:T(8,128)(2,1)S(1)} %get-tuple-element.38), channel_id=1, source_target_pairs={{0,8},{8,16},{16,24},{1,9},{9,17},{17,25},{2,10},{10,18},{18,26},{... | collective-permute-start | bytes 393224 | tf_op jit(solution)/shard_map/ppermute | solution.py:27
  22.9 7.0 %collective-permute-start.4 = (bf16[32,4,4,128]{3,0,2,1:T(8,128)(2,1)S(1)}, bf16[32,4,4,128]{3,0,2,1:T(8,128)(2,1)S(1)}, u32[]{:S(2)}, u32[]{:S(2)}) collective-permute-start(bf16[32,4,4,128]{3,0,2,1:T(8,128)(2,1)S(1)} %collective-permute-done.3), channel_id=1, source_target_pairs={{0,16},{8,24},{16,0},{24,8},{1,17},{9,25},{17,1},{25,9},{2,18},{10... | collective-permute-start | bytes 393224 | tf_op jit(solution)/shard_map/ppermute | solution.py:21
  30.1 5.4 %collective-permute-start.5 = (bf16[32,4,2,128]{3,0,2,1:T(8,128)(2,1)S(1)}, bf16[32,4,2,128]{3,0,2,1:T(8,128)(2,1)S(1)}, u32[]{:S(2)}, u32[]{:S(2)}) collective-permute-start(bf16[32,4,2,128]{3,0,2,1:T(8,128)(2,1)S(1)} %get-tuple-element.624), channel_id=1, source_target_pairs={{0,1},{1,2},{2,3},{3,4},{4,5},{5,6},{6,7},{8,9},{9,10},{10,11},{11... | collective-permute-start | bytes 196616 | tf_op jit(solution)/shard_map/ppermute | solution.py:12
  32.8 5.4 %collective-permute-start.6 = (bf16[32,4,2,128]{3,0,2,1:T(8,128)(2,1)S(1)}, bf16[32,4,2,128]{3,0,2,1:T(8,128)(2,1)S(1)}, u32[]{:S(2)}, u32[]{:S(2)}) collective-permute-start(bf16[32,4,2,128]{3,0,2,1:T(8,128)(2,1)S(1)} %get-tuple-element.625), channel_id=1, source_target_pairs={{1,0},{2,1},{3,2},{4,3},{5,4},{6,5},{7,6},{9,8},{10,9},{11,10},{12... | collective-permute-start | bytes 196616 | tf_op jit(solution)/shard_map/ppermute | solution.py:15
  34.3 15.3 %collective-permute-start.8 = (bf16[32,4,4,128]{3,0,2,1:T(8,128)(2,1)S(1)}, bf16[32,4,4,128]{3,0,2,1:T(8,128)(2,1)S(1)}, u32[]{:S(2)}, u32[]{:S(2)}) collective-permute-start(bf16[32,4,4,128]{3,0,2,1:T(8,128)(2,1)S(1)} %get-tuple-element.36), channel_id=1, source_target_pairs={{0,8},{8,0},{16,24},{24,16},{1,9},{9,1},{17,25},{25,17},{2,10},{10... | collective-permute-start | bytes 393224 | tf_op jit(solution)/shard_map/ppermute | solution.py:21
  46.2 11.4 %collective-permute-start.7 = (bf16[32,4,4,128]{3,0,2,1:T(8,128)(2,1)S(1)}, bf16[32,4,4,128]{3,0,2,1:T(8,128)(2,1)S(1)}, u32[]{:S(2)}, u32[]{:S(2)}) collective-permute-start(bf16[32,4,4,128]{3,0,2,1:T(8,128)(2,1)S(1)} %get-tuple-element.32), channel_id=1, source_target_pairs={{0,8},{8,16},{16,24},{1,9},{9,17},{17,25},{2,10},{10,18},{18,26},{... | collective-permute-start | bytes 393224 | tf_op jit(solution)/shard_map/ppermute | solution.py:27
  49.6 8.0 %collective-permute-start.9 = (bf16[32,4,4,128]{3,0,2,1:T(8,128)(2,1)S(1)}, bf16[32,4,4,128]{3,0,2,1:T(8,128)(2,1)S(1)}, u32[]{:S(2)}, u32[]{:S(2)}) collective-permute-start(bf16[32,4,4,128]{3,0,2,1:T(8,128)(2,1)S(1)} %collective-permute-done.8), channel_id=1, source_target_pairs={{0,16},{8,24},{16,0},{24,8},{1,17},{9,25},{17,1},{25,9},{2,18},{10... | collective-permute-start | bytes 393224 | tf_op jit(solution)/shard_map/ppermute | solution.py:21
  57.7 5.1 %collective-permute-start.10 = (bf16[32,4,2,128]{3,0,2,1:T(8,128)(2,1)S(1)}, bf16[32,4,2,128]{3,0,2,1:T(8,128)(2,1)S(1)}, u32[]{:S(2)}, u32[]{:S(2)}) collective-permute-start(bf16[32,4,2,128]{3,0,2,1:T(8,128)(2,1)S(1)} %get-tuple-element.622), channel_id=1, source_target_pairs={{0,1},{1,2},{2,3},{3,4},{4,5},{5,6},{6,7},{8,9},{9,10},{10,11},{11... | collective-permute-start | bytes 196616 | tf_op jit(solution)/shard_map/ppermute | solution.py:12
  60.3 5.5 %collective-permute-start.11 = (bf16[32,4,2,128]{3,0,2,1:T(8,128)(2,1)S(1)}, bf16[32,4,2,128]{3,0,2,1:T(8,128)(2,1)S(1)}, u32[]{:S(2)}, u32[]{:S(2)}) collective-permute-start(bf16[32,4,2,128]{3,0,2,1:T(8,128)(2,1)S(1)} %get-tuple-element.623), channel_id=1, source_target_pairs={{1,0},{2,1},{3,2},{4,3},{5,4},{6,5},{7,6},{9,8},{10,9},{11,10},{12... | collective-permute-start | bytes 196616 | tf_op jit(solution)/shard_map/ppermute | solution.py:15
  61.6 15.8 %collective-permute-start.13 = (bf16[32,4,4,128]{3,0,2,1:T(8,128)(2,1)S(1)}, bf16[32,4,4,128]{3,0,2,1:T(8,128)(2,1)S(1)}, u32[]{:S(2)}, u32[]{:S(2)}) collective-permute-start(bf16[32,4,4,128]{3,0,2,1:T(8,128)(2,1)S(1)} %get-tuple-element.30), channel_id=1, source_target_pairs={{0,8},{8,0},{16,24},{24,16},{1,9},{9,1},{17,25},{25,17},{2,10},{10... | collective-permute-start | bytes 393224 | tf_op jit(solution)/shard_map/ppermute | solution.py:21
  73.8 11.4 %collective-permute-start.12 = (bf16[32,4,4,128]{3,0,2,1:T(8,128)(2,1)S(1)}, bf16[32,4,4,128]{3,0,2,1:T(8,128)(2,1)S(1)}, u32[]{:S(2)}, u32[]{:S(2)}) collective-permute-start(bf16[32,4,4,128]{3,0,2,1:T(8,128)(2,1)S(1)} %get-tuple-element.26), channel_id=1, source_target_pairs={{0,8},{8,16},{16,24},{1,9},{9,17},{17,25},{2,10},{10,18},{18,26},{... | collective-permute-start | bytes 393224 | tf_op jit(solution)/shard_map/ppermute | solution.py:27
  77.4 7.7 %collective-permute-start.14 = (bf16[32,4,4,128]{3,0,2,1:T(8,128)(2,1)S(1)}, bf16[32,4,4,128]{3,0,2,1:T(8,128)(2,1)S(1)}, u32[]{:S(2)}, u32[]{:S(2)}) collective-permute-start(bf16[32,4,4,128]{3,0,2,1:T(8,128)(2,1)S(1)} %collective-permute-done.13), channel_id=1, source_target_pairs={{0,16},{8,24},{16,0},{24,8},{1,17},{9,25},{17,1},{25,9},{2,18},{10... | collective-permute-start | bytes 393224 | tf_op jit(solution)/shard_map/ppermute | solution.py:21
  85.3 5.5 %collective-permute-start.15 = (bf16[32,4,2,128]{3,0,2,1:T(8,128)(2,1)S(1)}, bf16[32,4,2,128]{3,0,2,1:T(8,128)(2,1)S(1)}, u32[]{:S(2)}, u32[]{:S(2)}) collective-permute-start(bf16[32,4,2,128]{3,0,2,1:T(8,128)(2,1)S(1)} %get-tuple-element.620), channel_id=1, source_target_pairs={{0,1},{1,2},{2,3},{3,4},{4,5},{5,6},{6,7},{8,9},{9,10},{10,11},{11... | collective-permute-start | bytes 196616 | tf_op jit(solution)/shard_map/ppermute | solution.py:12
  88.0 5.4 %collective-permute-start.16 = (bf16[32,4,2,128]{3,0,2,1:T(8,128)(2,1)S(1)}, bf16[32,4,2,128]{3,0,2,1:T(8,128)(2,1)S(1)}, u32[]{:S(2)}, u32[]{:S(2)}) collective-permute-start(bf16[32,4,2,128]{3,0,2,1:T(8,128)(2,1)S(1)} %get-tuple-element.621), channel_id=1, source_target_pairs={{1,0},{2,1},{3,2},{4,3},{5,4},{6,5},{7,6},{9,8},{10,9},{11,10},{12... | collective-permute-start | bytes 196616 | tf_op jit(solution)/shard_map/ppermute | solution.py:15
  89.3 12.7 %collective-permute-start.18 = (bf16[32,4,4,128]{3,0,2,1:T(8,128)(2,1)S(1)}, bf16[32,4,4,128]{3,0,2,1:T(8,128)(2,1)S(1)}, u32[]{:S(2)}, u32[]{:S(2)}) collective-permute-start(bf16[32,4,4,128]{3,0,2,1:T(8,128)(2,1)S(1)} %get-tuple-element.24), channel_id=1, source_target_pairs={{0,8},{8,0},{16,24},{24,16},{1,9},{9,1},{17,25},{25,17},{2,10},{10... | collective-permute-start | bytes 393224 | tf_op jit(solution)/shard_map/ppermute | solution.py:21
  102.0 5.5 %collective-permute-start.19 = (bf16[32,4,4,128]{3,0,2,1:T(8,128)(2,1)S(1)}, bf16[32,4,4,128]{3,0,2,1:T(8,128)(2,1)S(1)}, u32[]{:S(2)}, u32[]{:S(2)}) collective-permute-start(bf16[32,4,4,128]{3,0,2,1:T(8,128)(2,1)S(1)} %collective-permute-done.18), channel_id=1, source_target_pairs={{0,16},{8,24},{16,0},{24,8},{1,17},{9,25},{17,1},{25,9},{2,18},{10... | collective-permute-start | bytes 393224 | tf_op jit(solution)/shard_map/ppermute | solution.py:21
  104.6 3.8 %collective-permute-start.17 = (bf16[32,4,4,128]{3,0,2,1:T(8,128)(2,1)S(1)}, bf16[32,4,4,128]{3,0,2,1:T(8,128)(2,1)S(1)}, u32[]{:S(2)}, u32[]{:S(2)}) collective-permute-start(bf16[32,4,4,128]{3,0,2,1:T(8,128)(2,1)S(1)} %get-tuple-element.20), channel_id=1, source_target_pairs={{0,8},{8,16},{16,24},{1,9},{9,17},{17,25},{2,10},{10,18},{18,26},{... | collective-permute-start | bytes 393224 | tf_op jit(solution)/shard_map/ppermute | solution.py:27
  108.5 5.5 %collective-permute-start.20 = (bf16[32,4,2,128]{3,0,2,1:T(8,128)(2,1)S(1)}, bf16[32,4,2,128]{3,0,2,1:T(8,128)(2,1)S(1)}, u32[]{:S(2)}, u32[]{:S(2)}) collective-permute-start(bf16[32,4,2,128]{3,0,2,1:T(8,128)(2,1)S(1)} %get-tuple-element.618), channel_id=1, source_target_pairs={{0,1},{1,2},{2,3},{3,4},{4,5},{5,6},{6,7},{8,9},{9,10},{10,11},{11... | collective-permute-start | bytes 196616 | tf_op jit(solution)/shard_map/ppermute | solution.py:12
  112.6 4.2 %collective-permute-start.21 = (bf16[32,4,2,128]{3,0,2,1:T(8,128)(2,1)S(1)}, bf16[32,4,2,128]{3,0,2,1:T(8,128)(2,1)S(1)}, u32[]{:S(2)}, u32[]{:S(2)}) collective-permute-start(bf16[32,4,2,128]{3,0,2,1:T(8,128)(2,1)S(1)} %get-tuple-element.619), channel_id=1, source_target_pairs={{1,0},{2,1},{3,2},{4,3},{5,4},{6,5},{7,6},{9,8},{10,9},{11,10},{12... | collective-permute-start | bytes 196616 | tf_op jit(solution)/shard_map/ppermute | solution.py:15
  124.8 29.3 %collective-permute-start.22 = (bf16[32,4,1,128]{3,0,2,1:T(8,128)(2,1)S(1)}, bf16[32,4,1,128]{3,0,2,1:T(8,128)(2,1)S(1)}, u32[]{:S(2)}, u32[]{:S(2)}) collective-permute-start(bf16[32,4,1,128]{3,0,2,1:T(8,128)(2,1)S(1)} %get-tuple-element.616), channel_id=1, source_target_pairs={{0,1},{1,2},{2,3},{3,4},{4,5},{5,6},{6,7},{8,9},{9,10},{10,11},{11... | collective-permute-start | bytes 98312 | tf_op jit(solution)/shard_map/ppermute | solution.py:12
  129.6 24.4 %collective-permute-start.23 = (bf16[32,4,1,128]{3,0,2,1:T(8,128)(2,1)S(1)}, bf16[32,4,1,128]{3,0,2,1:T(8,128)(2,1)S(1)}, u32[]{:S(2)}, u32[]{:S(2)}) collective-permute-start(bf16[32,4,1,128]{3,0,2,1:T(8,128)(2,1)S(1)} %get-tuple-element.617), channel_id=1, source_target_pairs={{1,0},{2,1},{3,2},{4,3},{5,4},{6,5},{7,6},{9,8},{10,9},{11,10},{12... | collective-permute-start | bytes 98312 | tf_op jit(solution)/shard_map/ppermute | solution.py:15
  157.5 5.7 %collective-permute-start.24 = (bf16[32,4,1,128]{3,0,2,1:T(8,128)(2,1)S(1)}, bf16[32,4,1,128]{3,0,2,1:T(8,128)(2,1)S(1)}, u32[]{:S(2)}, u32[]{:S(2)}) collective-permute-start(bf16[32,4,1,128]{3,0,2,1:T(8,128)(2,1)S(1)} %get-tuple-element.614), channel_id=1, source_target_pairs={{0,1},{1,2},{2,3},{3,4},{4,5},{5,6},{6,7},{8,9},{9,10},{10,11},{11... | collective-permute-start | bytes 98312 | tf_op jit(solution)/shard_map/ppermute | solution.py:12
  160.6 3.9 %collective-permute-start.25 = (bf16[32,4,1,128]{3,0,2,1:T(8,128)(2,1)S(1)}, bf16[32,4,1,128]{3,0,2,1:T(8,128)(2,1)S(1)}, u32[]{:S(2)}, u32[]{:S(2)}) collective-permute-start(bf16[32,4,1,128]{3,0,2,1:T(8,128)(2,1)S(1)} %get-tuple-element.615), channel_id=1, source_target_pairs={{1,0},{2,1},{3,2},{4,3},{5,4},{6,5},{7,6},{9,8},{10,9},{11,10},{12... | collective-permute-start | bytes 98312 | tf_op jit(solution)/shard_map/ppermute | solution.py:15
  167.7 7.3 %collective-permute-start.26 = (bf16[32,4,4,128]{3,0,2,1:T(8,128)(2,1)S(1)}, bf16[32,4,4,128]{3,0,2,1:T(8,128)(2,1)S(1)}, u32[]{:S(2)}, u32[]{:S(2)}) collective-permute-start(bf16[32,4,4,128]{3,0,2,1:T(8,128)(2,1)S(1)} %get-tuple-element.16), channel_id=1, source_target_pairs={{8,0},{16,8},{24,16},{9,1},{17,9},{25,17},{10,2},{18,10},{26,18},{... | collective-permute-start | bytes 393224 | tf_op jit(solution)/shard_map/ppermute | solution.py:27
  169.0 13.7 %collective-permute-start.31 = (bf16[32,4,4,128]{3,0,2,1:T(8,128)(2,1)S(1)}, bf16[32,4,4,128]{3,0,2,1:T(8,128)(2,1)S(1)}, u32[]{:S(2)}, u32[]{:S(2)}) collective-permute-start(bf16[32,4,4,128]{3,0,2,1:T(8,128)(2,1)S(1)} %get-tuple-element.16), channel_id=1, source_target_pairs={{0,8},{8,0},{16,24},{24,16},{1,9},{9,1},{17,25},{25,17},{2,10},{10... | collective-permute-start | bytes 393224 | tf_op jit(solution)/shard_map/ppermute | solution.py:21
  175.1 11.0 %collective-permute-start.27 = (bf16[32,4,1,128]{3,0,2,1:T(8,128)(2,1)S(1)}, bf16[32,4,1,128]{3,0,2,1:T(8,128)(2,1)S(1)}, u32[]{:S(2)}, u32[]{:S(2)}) collective-permute-start(bf16[32,4,1,128]{3,0,2,1:T(8,128)(2,1)S(1)} %get-tuple-element.612), channel_id=1, source_target_pairs={{0,1},{1,2},{2,3},{3,4},{4,5},{5,6},{6,7},{8,9},{9,10},{10,11},{11... | collective-permute-start | bytes 98312 | tf_op jit(solution)/shard_map/ppermute | solution.py:12
  179.7 6.5 %collective-permute-start.28 = (bf16[32,4,1,128]{3,0,2,1:T(8,128)(2,1)S(1)}, bf16[32,4,1,128]{3,0,2,1:T(8,128)(2,1)S(1)}, u32[]{:S(2)}, u32[]{:S(2)}) collective-permute-start(bf16[32,4,1,128]{3,0,2,1:T(8,128)(2,1)S(1)} %get-tuple-element.613), channel_id=1, source_target_pairs={{1,0},{2,1},{3,2},{4,3},{5,4},{6,5},{7,6},{9,8},{10,9},{11,10},{12... | collective-permute-start | bytes 98312 | tf_op jit(solution)/shard_map/ppermute | solution.py:15
  182.8 18.1 %collective-permute-start.32 = (bf16[32,4,4,128]{3,0,2,1:T(8,128)(2,1)S(1)}, bf16[32,4,4,128]{3,0,2,1:T(8,128)(2,1)S(1)}, u32[]{:S(2)}, u32[]{:S(2)}) collective-permute-start(bf16[32,4,4,128]{3,0,2,1:T(8,128)(2,1)S(1)} %collective-permute-done.31), channel_id=1, source_target_pairs={{0,16},{8,24},{16,0},{24,8},{1,17},{9,25},{17,1},{25,9},{2,18},{10... | collective-permute-start | bytes 393224 | tf_op jit(solution)/shard_map/ppermute | solution.py:21
  189.5 6.3 %collective-permute-start.29 = (bf16[32,4,1,128]{3,0,2,1:T(8,128)(2,1)S(1)}, bf16[32,4,1,128]{3,0,2,1:T(8,128)(2,1)S(1)}, u32[]{:S(2)}, u32[]{:S(2)}) collective-permute-start(bf16[32,4,1,128]{3,0,2,1:T(8,128)(2,1)S(1)} %get-tuple-element.610), channel_id=1, source_target_pairs={{0,1},{1,2},{2,3},{3,4},{4,5},{5,6},{6,7},{8,9},{9,10},{10,11},{11... | collective-permute-start | bytes 98312 | tf_op jit(solution)/shard_map/ppermute | solution.py:12
  193.1 4.6 %collective-permute-start.30 = (bf16[32,4,1,128]{3,0,2,1:T(8,128)(2,1)S(1)}, bf16[32,4,1,128]{3,0,2,1:T(8,128)(2,1)S(1)}, u32[]{:S(2)}, u32[]{:S(2)}) collective-permute-start(bf16[32,4,1,128]{3,0,2,1:T(8,128)(2,1)S(1)} %get-tuple-element.611), channel_id=1, source_target_pairs={{1,0},{2,1},{3,2},{4,3},{5,4},{6,5},{7,6},{9,8},{10,9},{11,10},{12... | collective-permute-start | bytes 98312 | tf_op jit(solution)/shard_map/ppermute | solution.py:15
  201.1 14.1 %collective-permute-start.38 = (bf16[32,4,4,128]{3,0,2,1:T(8,128)(2,1)S(1)}, bf16[32,4,4,128]{3,0,2,1:T(8,128)(2,1)S(1)}, u32[]{:S(2)}, u32[]{:S(2)}) collective-permute-start(bf16[32,4,4,128]{3,0,2,1:T(8,128)(2,1)S(1)} %get-tuple-element.14), channel_id=1, source_target_pairs={{0,8},{8,0},{16,24},{24,16},{1,9},{9,1},{17,25},{25,17},{2,10},{10... | collective-permute-start | bytes 393224 | tf_op jit(solution)/shard_map/ppermute | solution.py:21
  201.2 8.3 %collective-permute-start.33 = (bf16[32,4,4,128]{3,0,2,1:T(8,128)(2,1)S(1)}, bf16[32,4,4,128]{3,0,2,1:T(8,128)(2,1)S(1)}, u32[]{:S(2)}, u32[]{:S(2)}) collective-permute-start(bf16[32,4,4,128]{3,0,2,1:T(8,128)(2,1)S(1)} %fusion.276), channel_id=1, source_target_pairs={{8,0},{16,8},{24,16},{9,1},{17,9},{25,17},{10,2},{18,10},{26,18},{... | collective-permute-start | bytes 393224 | tf_op jit(solution)/shard_map/ppermute | solution.py:27
  209.7 6.2 %collective-permute-start.34 = (bf16[32,4,1,128]{3,0,2,1:T(8,128)(2,1)S(1)}, bf16[32,4,1,128]{3,0,2,1:T(8,128)(2,1)S(1)}, u32[]{:S(2)}, u32[]{:S(2)}) collective-permute-start(bf16[32,4,1,128]{3,0,2,1:T(8,128)(2,1)S(1)} %get-tuple-element.608), channel_id=1, source_target_pairs={{0,1},{1,2},{2,3},{3,4},{4,5},{5,6},{6,7},{8,9},{9,10},{10,11},{11... | collective-permute-start | bytes 98312 | tf_op jit(solution)/shard_map/ppermute | solution.py:12
  212.5 4.0 %collective-permute-start.35 = (bf16[32,4,1,128]{3,0,2,1:T(8,128)(2,1)S(1)}, bf16[32,4,1,128]{3,0,2,1:T(8,128)(2,1)S(1)}, u32[]{:S(2)}, u32[]{:S(2)}) collective-permute-start(bf16[32,4,1,128]{3,0,2,1:T(8,128)(2,1)S(1)} %get-tuple-element.609), channel_id=1, source_target_pairs={{1,0},{2,1},{3,2},{4,3},{5,4},{6,5},{7,6},{9,8},{10,9},{11,10},{12... | collective-permute-start | bytes 98312 | tf_op jit(solution)/shard_map/ppermute | solution.py:15
  215.2 15.7 %collective-permute-start.39 = (bf16[32,4,4,128]{3,0,2,1:T(8,128)(2,1)S(1)}, bf16[32,4,4,128]{3,0,2,1:T(8,128)(2,1)S(1)}, u32[]{:S(2)}, u32[]{:S(2)}) collective-permute-start(bf16[32,4,4,128]{3,0,2,1:T(8,128)(2,1)S(1)} %collective-permute-done.38), channel_id=1, source_target_pairs={{0,16},{8,24},{16,0},{24,8},{1,17},{9,25},{17,1},{25,9},{2,18},{10... | collective-permute-start | bytes 393224 | tf_op jit(solution)/shard_map/ppermute | solution.py:21
  219.8 7.7 %collective-permute-start.36 = (bf16[32,4,1,128]{3,0,2,1:T(8,128)(2,1)S(1)}, bf16[32,4,1,128]{3,0,2,1:T(8,128)(2,1)S(1)}, u32[]{:S(2)}, u32[]{:S(2)}) collective-permute-start(bf16[32,4,1,128]{3,0,2,1:T(8,128)(2,1)S(1)} %get-tuple-element.606), channel_id=1, source_target_pairs={{0,1},{1,2},{2,3},{3,4},{4,5},{5,6},{6,7},{8,9},{9,10},{10,11},{11... | collective-permute-start | bytes 98312 | tf_op jit(solution)/shard_map/ppermute | solution.py:12
  224.7 3.1 collective-permute-start.37
  231.1 14.7 %collective-permute-start.45 = (bf16[32,4,4,128]{3,0,2,1:T(8,128)(2,1)S(1)}, bf16[32,4,4,128]{3,0,2,1:T(8,128)(2,1)S(1)}, u32[]{:S(2)}, u32[]{:S(2)}) collective-permute-start(bf16[32,4,4,128]{3,0,2,1:T(8,128)(2,1)S(1)} %get-tuple-element.12), channel_id=1, source_target_pairs={{0,8},{8,0},{16,24},{24,16},{1,9},{9,1},{17,25},{25,17},{2,10},{10... | collective-permute-start | bytes 393224 | tf_op jit(solution)/shard_map/ppermute | solution.py:21
  233.0 7.4 %collective-permute-start.40 = (bf16[32,4,4,128]{3,0,2,1:T(8,128)(2,1)S(1)}, bf16[32,4,4,128]{3,0,2,1:T(8,128)(2,1)S(1)}, u32[]{:S(2)}, u32[]{:S(2)}) collective-permute-start(bf16[32,4,4,128]{3,0,2,1:T(8,128)(2,1)S(1)} %fusion.275), channel_id=1, source_target_pairs={{8,0},{16,8},{24,16},{9,1},{17,9},{25,17},{10,2},{18,10},{26,18},{... | collective-permute-start | bytes 393224 | tf_op jit(solution)/shard_map/ppermute | solution.py:27
  240.5 6.5 %collective-permute-start.41 = (bf16[32,4,1,128]{3,0,2,1:T(8,128)(2,1)S(1)}, bf16[32,4,1,128]{3,0,2,1:T(8,128)(2,1)S(1)}, u32[]{:S(2)}, u32[]{:S(2)}) collective-permute-start(bf16[32,4,1,128]{3,0,2,1:T(8,128)(2,1)S(1)} %get-tuple-element.604), channel_id=1, source_target_pairs={{0,1},{1,2},{2,3},{3,4},{4,5},{5,6},{6,7},{8,9},{9,10},{10,11},{11... | collective-permute-start | bytes 98312 | tf_op jit(solution)/shard_map/ppermute | solution.py:12
  243.1 3.8 %collective-permute-start.42 = (bf16[32,4,1,128]{3,0,2,1:T(8,128)(2,1)S(1)}, bf16[32,4,1,128]{3,0,2,1:T(8,128)(2,1)S(1)}, u32[]{:S(2)}, u32[]{:S(2)}) collective-permute-start(bf16[32,4,1,128]{3,0,2,1:T(8,128)(2,1)S(1)} %get-tuple-element.605), channel_id=1, source_target_pairs={{1,0},{2,1},{3,2},{4,3},{5,4},{6,5},{7,6},{9,8},{10,9},{11,10},{12... | collective-permute-start | bytes 98312 | tf_op jit(solution)/shard_map/ppermute | solution.py:15
  245.8 15.9 %collective-permute-start.46 = (bf16[32,4,4,128]{3,0,2,1:T(8,128)(2,1)S(1)}, bf16[32,4,4,128]{3,0,2,1:T(8,128)(2,1)S(1)}, u32[]{:S(2)}, u32[]{:S(2)}) collective-permute-start(bf16[32,4,4,128]{3,0,2,1:T(8,128)(2,1)S(1)} %collective-permute-done.45), channel_id=1, source_target_pairs={{0,16},{8,24},{16,0},{24,8},{1,17},{9,25},{17,1},{25,9},{2,18},{10... | collective-permute-start | bytes 393224 | tf_op jit(solution)/shard_map/ppermute | solution.py:21
  250.3 7.1 %collective-permute-start.43 = (bf16[32,4,1,128]{3,0,2,1:T(8,128)(2,1)S(1)}, bf16[32,4,1,128]{3,0,2,1:T(8,128)(2,1)S(1)}, u32[]{:S(2)}, u32[]{:S(2)}) collective-permute-start(bf16[32,4,1,128]{3,0,2,1:T(8,128)(2,1)S(1)} %get-tuple-element.602), channel_id=1, source_target_pairs={{0,1},{1,2},{2,3},{3,4},{4,5},{5,6},{6,7},{8,9},{9,10},{10,11},{11... | collective-permute-start | bytes 98312 | tf_op jit(solution)/shard_map/ppermute | solution.py:12
  254.8 3.8 %collective-permute-start.44 = (bf16[32,4,1,128]{3,0,2,1:T(8,128)(2,1)S(1)}, bf16[32,4,1,128]{3,0,2,1:T(8,128)(2,1)S(1)}, u32[]{:S(2)}, u32[]{:S(2)}) collective-permute-start(bf16[32,4,1,128]{3,0,2,1:T(8,128)(2,1)S(1)} %get-tuple-element.603), channel_id=1, source_target_pairs={{1,0},{2,1},{3,2},{4,3},{5,4},{6,5},{7,6},{9,8},{10,9},{11,10},{12... | collective-permute-start | bytes 98312 | tf_op jit(solution)/shard_map/ppermute | solution.py:15
  261.7 5.1 %copy-start.1 = (bf16[2,32,4,4,128]{4,1,3,2,0:T(8,128)(2,1)}, bf16[2,32,4,4,128]{4,1,3,2,0:T(8,128)(2,1)S(1)}, u32[]{:S(2)}) copy-start(bf16[2,32,4,4,128]{4,1,3,2,0:T(8,128)(2,1)S(1)} %bitcast_dynamic-update-slice_fusion.10) | copy-start | bytes 786436
  261.9 5.6 %copy-start.3 = (f32[2,32,4,4,128]{4,1,3,2,0:T(8,128)}, f32[2,32,4,4,128]{4,1,3,2,0:T(8,128)S(1)}, u32[]{:S(2)}) copy-start(f32[2,32,4,4,128]{4,1,3,2,0:T(8,128)S(1)} %get-tuple-element.9) | copy-start | bytes 1572868
  261.9 6.9 %collective-permute-start.47 = (bf16[32,4,4,128]{3,0,2,1:T(8,128)(2,1)S(1)}, bf16[32,4,4,128]{3,0,2,1:T(8,128)(2,1)S(1)}, u32[]{:S(2)}, u32[]{:S(2)}) collective-permute-start(bf16[32,4,4,128]{3,0,2,1:T(8,128)(2,1)S(1)} %fusion.274), channel_id=1, source_target_pairs={{8,0},{16,8},{24,16},{9,1},{17,9},{25,17},{10,2},{18,10},{26,18},{... | collective-permute-start | bytes 393224 | tf_op jit(solution)/shard_map/ppermute | solution.py:27
  263.3 13.2 %collective-permute-start.52 = (bf16[32,4,4,128]{3,0,2,1:T(8,128)(2,1)S(1)}, bf16[32,4,4,128]{3,0,2,1:T(8,128)(2,1)}, u32[]{:S(2)}, u32[]{:S(2)}) collective-permute-start(bf16[32,4,4,128]{3,0,2,1:T(8,128)(2,1)S(1)} %get-tuple-element.10), channel_id=1, source_target_pairs={{0,8},{8,0},{16,24},{24,16},{1,9},{9,1},{17,25},{25,17},{2,10},{10... | collective-permute-start | bytes 393224 | tf_op jit(solution)/shard_map/ppermute | solution.py:21
  269.0 8.1 %collective-permute-start.48 = (bf16[32,4,1,128]{3,0,2,1:T(8,128)(2,1)S(1)}, bf16[32,4,1,128]{3,0,2,1:T(8,128)(2,1)S(1)}, u32[]{:S(2)}, u32[]{:S(2)}) collective-permute-start(bf16[32,4,1,128]{3,0,2,1:T(8,128)(2,1)S(1)} %get-tuple-element.600), channel_id=1, source_target_pairs={{0,1},{1,2},{2,3},{3,4},{4,5},{5,6},{6,7},{8,9},{9,10},{10,11},{11... | collective-permute-start | bytes 98312 | tf_op jit(solution)/shard_map/ppermute | solution.py:12
  273.6 3.9 %collective-permute-start.49 = (bf16[32,4,1,128]{3,0,2,1:T(8,128)(2,1)S(1)}, bf16[32,4,1,128]{3,0,2,1:T(8,128)(2,1)S(1)}, u32[]{:S(2)}, u32[]{:S(2)}) collective-permute-start(bf16[32,4,1,128]{3,0,2,1:T(8,128)(2,1)S(1)} %get-tuple-element.601), channel_id=1, source_target_pairs={{1,0},{2,1},{3,2},{4,3},{5,4},{6,5},{7,6},{9,8},{10,9},{11,10},{12... | collective-permute-start | bytes 98312 | tf_op jit(solution)/shard_map/ppermute | solution.py:15
  276.5 56.6 %collective-permute-start.53 = (bf16[32,4,4,128]{3,0,2,1:T(8,128)(2,1)}, bf16[32,4,4,128]{3,0,2,1:T(8,128)(2,1)}, u32[]{:S(2)}, u32[]{:S(2)}) collective-permute-start(bf16[32,4,4,128]{3,0,2,1:T(8,128)(2,1)} %collective-permute-done.52), channel_id=1, source_target_pairs={{0,16},{8,24},{16,0},{24,8},{1,17},{9,25},{17,1},{25,9},{2,18},{10... | collective-permute-start | bytes 393224 | tf_op jit(solution)/shard_map/ppermute | solution.py:21
  280.8 8.0 %copy-start.5 = (bf16[32,4,4,128]{3,0,2,1:T(8,128)(2,1)}, bf16[32,4,4,128]{3,0,2,1:T(8,128)(2,1)S(1)}, u32[]{:S(2)}) copy-start(bf16[32,4,4,128]{3,0,2,1:T(8,128)(2,1)S(1)} %fusion.185) | copy-start | bytes 393220
  281.5 46.2 %collective-permute-start.50 = (bf16[32,4,1,128]{3,0,2,1:T(8,128)(2,1)}, bf16[32,4,1,128]{3,0,2,1:T(8,128)(2,1)}, u32[]{:S(2)}, u32[]{:S(2)}) collective-permute-start(bf16[32,4,1,128]{3,0,2,1:T(8,128)(2,1)} %get-tuple-element.598), channel_id=1, source_target_pairs={{0,1},{1,2},{2,3},{3,4},{4,5},{5,6},{6,7},{8,9},{9,10},{10,11},{11... | collective-permute-start | bytes 98312 | tf_op jit(solution)/shard_map/ppermute | solution.py:12
  286.6 41.1 %collective-permute-start.51 = (bf16[32,4,1,128]{3,0,2,1:T(8,128)(2,1)}, bf16[32,4,1,128]{3,0,2,1:T(8,128)(2,1)}, u32[]{:S(2)}, u32[]{:S(2)}) collective-permute-start(bf16[32,4,1,128]{3,0,2,1:T(8,128)(2,1)} %get-tuple-element.599), channel_id=1, source_target_pairs={{1,0},{2,1},{3,2},{4,3},{5,4},{6,5},{7,6},{9,8},{10,9},{11,10},{12... | collective-permute-start | bytes 98312 | tf_op jit(solution)/shard_map/ppermute | solution.py:15
  325.7 2.1 copy-start.6
  330.7 1.3 copy-start.11
  332.8 1.2 copy-start.4
  332.8 1.3 copy-start.7
  (2 other events, 2.0 us)
